TPU v7x, 512 devices: a whole 4x8x8 slice. The times are simulated.
512 devices in a mesh: cell: 32 (over y, z_hi), sensor: 16 (over z_lo, x, core).
Axes of the slice: x: 4, y: 8, z: 8 (z_hi: 4, z_lo: 2; z = z_hi * 2 + z_lo), core: 2. Of those that a mesh axis runs over, the one named last changes fastest.
Arguments:
- kernel: bfloat16 [2, 65, 1024, 8192], P(None, None, 'sensor', 'cell'), may hold values from -3 to 3
- observed: float32 [64, 1024], P(None, 'sensor'), may hold values from -6 to 6
- start_model: float32 [64, 8192], P(None, 'cell'), may hold values from -6 to 6
- start_multiplier: float32 [4, 64, 8192], P(None, None, 'cell'), may hold values from -1.8 to 1.8
- neighbours: int32 [4, 8192], P(None, 'cell'), may hold values from 0 to 8191, as said below
- tile_of_cell: int32 [8192], P('cell'), may hold values from 0 to 63
- tile_weight: float32 [64], replicated, may hold values from 0.3 to 3
Outputs:
- estimate: float32 [64, 8192], P(None, 'cell')
- auxiliary: float32 [4, 64, 8192], P(None, None, 'cell')
- multiplier: float32 [4, 64, 8192], P(None, None, 'cell')
Inputs may be any that keep to these rules, and one draw needn't show every extreme that they name: The cells form a grid of 64 rows of 128 cells, numbered row by row. neighbours[k, c] is c itself or the cell beside c: c + 1 for k = 0 and c - 1 for k = 1 within the same row, c - 128 for k = 2 and c + 128 for k = 3. Where neighbours[k, c] = c' differs from c, neighbours[k xor 1, c'] = c.
All inputs are finite; a program needn't handle non-finite values.
Results may differ from a plain program's by a relative error of at most 0.00092.
Values sent between devices are 32-bit elements; how exact they have to be, the bound alone decides.
A program may use at most 64 MiB of HBM per device.

v0:
```python
import functools

import jax
import jax.numpy as jnp
from jax import lax
from jax.sharding import Mesh
from jax.sharding import PartitionSpec as P

COLS = 128
ITERS = 2
CELL = ("cell_0", "cell_1")


SHRINK_SCALE = 0.4
TINY = 1e-06


def padded_2(array, sides, width):
    for axis, dim in sides:
        devices, length = (lax.axis_size(axis), array.shape[dim])
        up = [(i, (i + 1) % devices) for i in range(devices - 1)]
        down = [(j, i) for i, j in up]
        last = lax.slice_in_dim(array, length - width, length, axis=dim)
        leading = lax.slice_in_dim(array, 0, width, axis=dim)
        before = lax.ppermute(last, axis, up)
        after = lax.ppermute(leading, axis, down)
        array = jnp.concatenate([before, array, after], axis=dim)
    return array


def sent_to_all(array, axis):
    devices = lax.axis_size(axis)
    return lax.all_to_all(
        jnp.broadcast_to(array[None], (devices, *array.shape)), axis, 0, 0, tiled=True
    )


def taken_together(array, axis):
    return sent_to_all(array, axis).sum(axis=0)


def by_axis(array, axes):
    return functools.reduce(lax.psum, axes, array)


def exact_dot(left, right):
    return jnp.dot(left, right, precision=lax.Precision.HIGHEST, preferred_element_type=jnp.float32)


def tables(times_count, freq_count):
    padded = 2 * times_count
    freq_index = lax.broadcasted_iota(jnp.int32, (freq_count, times_count), 0)
    time_index = lax.broadcasted_iota(jnp.int32, (freq_count, times_count), 1)
    phase = (freq_index * time_index % padded).astype(jnp.float32) * (2.0 * jnp.pi / padded)
    cosine = jnp.cos(phase)
    sine_table = jnp.sin(phase)
    weight = (
        jnp.where((freq_index == 0) | (freq_index == freq_count - 1), 1.0, 2.0).astype(jnp.float32)
        / padded
    )
    return (cosine, sine_table, cosine * weight, sine_table * weight)


def batched(matrix, vector):
    return jnp.einsum("fsc,fc->fs", matrix, vector, preferred_element_type=jnp.float32)


def transposed(matrix, vector):
    return jnp.einsum("fsc,fs->fc", matrix, vector, preferred_element_type=jnp.float32)


def with_rims(values):
    return padded_2(values, ((CELL, 2),), COLS)


def penalty_margins(penalty):
    return with_rims(penalty)


def differences(extended, local_index, center):
    taken = [jnp.take(extended[0], local_index[direction], axis=1) for direction in range(4)]
    return jnp.stack(taken) - center[None]


def divergence(extended, local_index, linked, own):
    accumulated = jnp.zeros(own.shape[1:], jnp.float32)
    for direction in range(4):
        partner = direction ^ 1
        arriving = jnp.take(extended[direction], local_index[partner], axis=1)
        accumulated = accumulated + linked[partner] * arriving - linked[direction] * own[direction]
    return accumulated


def per_device(
    kernel, observed, start_model, start_multiplier, neighbours, tile_of_cell, tile_weight
):
    times_count = start_model.shape[0]
    freq_count = kernel.shape[1]
    cell_count = start_model.shape[1]
    cosine, sine_table, cos_weighted, sin_weighted = tables(times_count, freq_count)
    offset = lax.axis_index(CELL) * cell_count
    own_cells = offset + lax.broadcasted_iota(jnp.int32, (1, cell_count), 1)
    linked = (neighbours != own_cells).astype(jnp.float32)
    local_index = neighbours - offset + COLS
    labels = lax.broadcasted_iota(jnp.int32, (tile_weight.shape[0], cell_count), 0)
    threshold = SHRINK_SCALE * jnp.sum(
        jnp.where(labels == tile_of_cell[None, :], tile_weight[:, None], 0.0), axis=0
    )

    def synthesis(out_real, out_imag):
        return exact_dot(cos_weighted.T, out_real) - exact_dot(sin_weighted.T, out_imag)

    def forward(series):
        real_part = exact_dot(cosine, series).astype(jnp.bfloat16)
        imag_part = (-exact_dot(sine_table, series)).astype(jnp.bfloat16)
        out_real = batched(kernel[0], real_part) - batched(kernel[1], imag_part)
        out_imag = batched(kernel[0], imag_part) + batched(kernel[1], real_part)
        return taken_together(synthesis(out_real, out_imag), CELL)

    estimate = start_model
    multiplier = start_multiplier
    predicted = forward(estimate)
    model_jumps = differences(with_rims(estimate[None]), local_index, estimate)
    auxiliary = model_jumps
    for iteration in range(ITERS):
        penalty = model_jumps - auxiliary + multiplier
        misfit = predicted - observed
        back_real = exact_dot(cos_weighted, misfit).astype(jnp.bfloat16)
        back_imag = (-exact_dot(sin_weighted, misfit)).astype(jnp.bfloat16)
        adjoint_spec_real = transposed(kernel[0], back_real) + transposed(kernel[1], back_imag)
        adjoint_spec_imag = transposed(kernel[0], back_imag) - transposed(kernel[1], back_real)
        gradient = taken_together(
            exact_dot(cosine.T, adjoint_spec_real) - exact_dot(sine_table.T, adjoint_spec_imag),
            "sensor",
        ) + divergence(penalty_margins(penalty), local_index, linked, penalty)
        response = forward(gradient)
        grad_jumps = differences(with_rims(gradient[None]), local_index, gradient)
        grad_square = jnp.sum(gradient * gradient)
        jump_square = jnp.sum(grad_jumps * grad_jumps)
        response_square = jnp.sum(response * response)
        grad_square, jump_square = (by_axis(grad_square, CELL), by_axis(jump_square, CELL))
        response_square = taken_together(response_square, "sensor")
        step_size = grad_square / (response_square + jump_square + TINY)
        estimate = estimate - step_size * gradient
        predicted = predicted - step_size * response
        model_jumps = model_jumps - step_size * grad_jumps
        shifted = model_jumps + multiplier
        auxiliary = jnp.sign(shifted) * jnp.maximum(jnp.abs(shifted) - threshold, 0.0)
        multiplier = shifted - auxiliary
    return (estimate, auxiliary, multiplier)


def solution(mesh):
    split = Mesh(mesh.devices.reshape(8, 4, mesh.shape["sensor"]), ("cell_0", "cell_1", "sensor"))
    in_specs = (
        P(None, None, "sensor", CELL),
        P(None, "sensor"),
        P(None, CELL),
        P(None, None, CELL),
        P(None, CELL),
        P(CELL),
        P(),
    )
    out_specs = (P(None, CELL), P(None, None, CELL), P(None, None, CELL))
    return jax.shard_map(
        per_device, mesh=split, in_specs=in_specs, out_specs=out_specs, check_vma=False
    )
```

profile of v0, /device:TPU:1, one launch (start us, length us, event | category | flops | bytes accessed | tf_op | source)
XLA Modules:
  0.0 303.4 jit_solution(4559042784049680668)
XLA Ops:
  11.5 16.5 %all-to-all-start = ((f32[32,1,4096]{2,1,0:T(1,128)}), f32[32,1,4096]{2,1,0:T(1,128)S(1)}, u32[]{:S(2)}, u32[]{:S(2)}) async-start(f32[32,1,4096]{2,1,0:T(1,128)} %reshape.285), calls=%async_computation | async-start | bytes 1048576 | tf_op jit(solution)/shard_map/all_to_all | solution.py:33
  29.4 4.9 %collective-permute-start = (f32[1,64,128]{1,2,0:T(8,128)S(1)}, f32[1,64,128]{1,2,0:T(8,128)S(1)}, u32[]{:S(2)}, u32[]{:S(2)}) collective-permute-start(f32[1,64,128]{1,2,0:T(8,128)S(1)} %get-tuple-element.43), channel_id=1, source_target_pairs={{0,16},{16,32},{32,48},{48,64},{64,80},{80,96},{96,112},{112,128},... | collective-permute-start | bytes 98312 | tf_op jit(solution)/shard_map/ppermute | solution.py:25
  34.5 10.6 %all-to-all-done = f32[32,1,4096]{2,1,0:T(1,128)S(1)} async-done(((f32[32,1,4096]{2,1,0:T(1,128)}), f32[32,1,4096]{2,1,0:T(1,128)S(1)}, u32[]{:S(2)}, u32[]{:S(2)}) %all-to-all-start) | async-done | bytes 524320 | tf_op jit(solution)/shard_map/all_to_all | solution.py:33
  59.1 8.2 %all-to-all-start.1 = ((f32[16,64,256]{2,1,0:T(8,128)}), f32[16,64,256]{2,1,0:T(8,128)S(1)}, u32[]{:S(2)}, u32[]{:S(2)}) async-start(f32[16,64,256]{2,1,0:T(8,128)} %broadcast_in_dim.52), calls=%async_computation.1 | async-start | bytes 2097152 | tf_op jit(solution)/shard_map/all_to_all | solution.py:33
  72.3 5.1 %collective-permute-start.2 = (f32[4,64,128]{1,2,0:T(8,128)S(1)}, f32[4,64,128]{1,2,0:T(8,128)S(1)}, u32[]{:S(2)}, u32[]{:S(2)}) collective-permute-start(f32[4,64,128]{1,2,0:T(8,128)S(1)} %get-tuple-element.37), channel_id=1, source_target_pairs={{0,16},{16,32},{32,48},{48,64},{64,80},{80,96},{96,112},{112,128},... | collective-permute-start | bytes 393224 | tf_op jit(solution)/shard_map/ppermute | solution.py:25
  78.0 6.6 %collective-permute-done.3 = f32[4,64,128]{1,2,0:T(8,128)S(1)} collective-permute-done((f32[4,64,128]{1,2,0:T(8,128)S(1)}, f32[4,64,128]{1,2,0:T(8,128)S(1)}, u32[]{:S(2)}, u32[]{:S(2)}) %collective-permute-start.3) | collective-permute-done | bytes 131104 | tf_op jit(solution)/shard_map/ppermute | solution.py:26
  88.5 5.7 %all-to-all-done.1 = f32[16,64,256]{2,1,0:T(8,128)S(1)} async-done(((f32[16,64,256]{2,1,0:T(8,128)}), f32[16,64,256]{2,1,0:T(8,128)S(1)}, u32[]{:S(2)}, u32[]{:S(2)}) %all-to-all-start.1) | async-done | bytes 1048608 | tf_op jit(solution)/shard_map/all_to_all | solution.py:33
  99.4 2.3 fusion.8
  106.0 4.9 %collective-permute-start.4 = (f32[1,64,128]{1,2,0:T(8,128)S(1)}, f32[1,64,128]{1,2,0:T(8,128)S(1)}, u32[]{:S(2)}, u32[]{:S(2)}) collective-permute-start(f32[1,64,128]{1,2,0:T(8,128)S(1)} %get-tuple-element.41), channel_id=1, source_target_pairs={{0,16},{16,32},{32,48},{48,64},{64,80},{80,96},{96,112},{112,128},... | collective-permute-start | bytes 98312 | tf_op jit(solution)/shard_map/ppermute | solution.py:25
  113.3 9.6 %all-to-all-start.2 = ((f32[32,1,4096]{2,1,0:T(1,128)}), f32[32,1,4096]{2,1,0:T(1,128)S(1)}, u32[]{:S(2)}, u32[]{:S(2)}) async-start(f32[32,1,4096]{2,1,0:T(1,128)} %reshape.287), calls=%async_computation.2 | async-start | bytes 1048576 | tf_op jit(solution)/shard_map/all_to_all | solution.py:33
  127.1 15.8 %all-reduce.1 = (f32[]{:T(128)}, f32[]{:T(128)}) all-reduce(f32[]{:T(128)} %get-tuple-element.25, f32[]{:T(128)} %multiply_reduce_fusion.1), channel_id=1, replica_groups=mesh['cell_0'=8,'cell_1'=4,'sensor'=16] {'cell_0'}, use_global_device_ids=true, to_apply=%region_3.5 | all-reduce | flops 2 | bytes 16 | tf_op jit(solution)/shard_map/psum | solution.py:43
  147.3 11.5 %all-to-all-start.3 = ((f32[16,1,1]{2,1,0:T(1,128)}), f32[16,1,1]{2,1,0:T(1,128)S(1)}, u32[]{:S(2)}, u32[]{:S(2)}) async-start(f32[16,1,1]{2,1,0:T(1,128)} %broadcast_in_dim.55), calls=%async_computation.3 | async-start | bytes 16384 | tf_op jit(solution)/shard_map/all_to_all | solution.py:33
  158.8 10.7 %all-reduce.3 = (f32[]{:T(128)}, f32[]{:T(128)}) all-reduce(f32[]{:T(128)} %get-tuple-element.15, f32[]{:T(128)} %get-tuple-element.16), channel_id=1, replica_groups=mesh['cell_0'=8,'cell_1'=4,'sensor'=16] {'cell_1'}, use_global_device_ids=true, to_apply=%region_4.6 | all-reduce | flops 2 | bytes 16 | tf_op jit(solution)/shard_map/psum | solution.py:43
  183.1 7.8 %all-to-all-start.4 = ((f32[16,64,256]{2,1,0:T(8,128)}), f32[16,64,256]{2,1,0:T(8,128)S(1)}, u32[]{:S(2)}, u32[]{:S(2)}) async-start(f32[16,64,256]{2,1,0:T(8,128)} %broadcast_in_dim.95), calls=%async_computation.4 | async-start | bytes 2097152 | tf_op jit(solution)/shard_map/all_to_all | solution.py:33
  192.8 4.9 %collective-permute-start.6 = (f32[4,64,128]{1,2,0:T(8,128)S(1)}, f32[4,64,128]{1,2,0:T(8,128)S(1)}, u32[]{:S(2)}, u32[]{:S(2)}) collective-permute-start(f32[4,64,128]{1,2,0:T(8,128)S(1)} %get-tuple-element.35), channel_id=1, source_target_pairs={{0,16},{16,32},{32,48},{48,64},{64,80},{80,96},{96,112},{112,128},... | collective-permute-start | bytes 393224 | tf_op jit(solution)/shard_map/ppermute | solution.py:25
  197.7 7.3 %collective-permute-done.7 = f32[4,64,128]{1,2,0:T(8,128)S(1)} collective-permute-done((f32[4,64,128]{1,2,0:T(8,128)S(1)}, f32[4,64,128]{1,2,0:T(8,128)S(1)}, u32[]{:S(2)}, u32[]{:S(2)}) %collective-permute-start.7) | collective-permute-done | bytes 131104 | tf_op jit(solution)/shard_map/ppermute | solution.py:26
  205.0 3.4 %collective-permute-done.6 = f32[4,64,128]{1,2,0:T(8,128)S(1)} collective-permute-done((f32[4,64,128]{1,2,0:T(8,128)S(1)}, f32[4,64,128]{1,2,0:T(8,128)S(1)}, u32[]{:S(2)}, u32[]{:S(2)}) %collective-permute-start.6) | collective-permute-done | bytes 131104 | tf_op jit(solution)/shard_map/ppermute | solution.py:25
  209.2 2.3 gather_fusion.15
  214.3 3.4 %all-to-all-done.4 = f32[16,64,256]{2,1,0:T(8,128)S(1)} async-done(((f32[16,64,256]{2,1,0:T(8,128)}), f32[16,64,256]{2,1,0:T(8,128)S(1)}, u32[]{:S(2)}, u32[]{:S(2)}) %all-to-all-start.4) | async-done | bytes 1048608 | tf_op jit(solution)/shard_map/all_to_all | solution.py:33
  229.6 5.5 %collective-permute-start.8 = (f32[1,64,128]{1,2,0:T(8,128)S(1)}, f32[1,64,128]{1,2,0:T(8,128)S(1)}, u32[]{:S(2)}, u32[]{:S(2)}) collective-permute-start(f32[1,64,128]{1,2,0:T(8,128)S(1)} %get-tuple-element.39), channel_id=1, source_target_pairs={{0,16},{16,32},{32,48},{48,64},{64,80},{80,96},{96,112},{112,128},... | collective-permute-start | bytes 98312 | tf_op jit(solution)/shard_map/ppermute | solution.py:25
  237.5 12.7 %all-to-all-start.5 = ((f32[32,1,4096]{2,1,0:T(1,128)}), f32[32,1,4096]{2,1,0:T(1,128)S(1)}, u32[]{:S(2)}, u32[]{:S(2)}) async-start(f32[32,1,4096]{2,1,0:T(1,128)} %reshape.289), calls=%async_computation.5 | async-start | bytes 1048576 | tf_op jit(solution)/shard_map/all_to_all | solution.py:33
  257.1 14.8 %all-reduce = (f32[]{:T(128)}, f32[]{:T(128)}) all-reduce(f32[]{:T(128)} %get-tuple-element.23, f32[]{:T(128)} %multiply_reduce_fusion), channel_id=1, replica_groups=mesh['cell_0'=8,'cell_1'=4,'sensor'=16] {'cell_0'}, use_global_device_ids=true, to_apply=%region_14.16 | all-reduce | flops 2 | bytes 16 | tf_op jit(solution)/shard_map/psum | solution.py:43
  276.3 9.4 %all-to-all-start.6 = ((f32[16,1,1]{2,1,0:T(1,128)}), f32[16,1,1]{2,1,0:T(1,128)S(1)}, u32[]{:S(2)}, u32[]{:S(2)}) async-start(f32[16,1,1]{2,1,0:T(1,128)} %broadcast_in_dim.99), calls=%async_computation.6 | async-start | bytes 16384 | tf_op jit(solution)/shard_map/all_to_all | solution.py:33
  285.6 10.8 %all-reduce.2 = (f32[]{:T(128)}, f32[]{:T(128)}) all-reduce(f32[]{:T(128)} %get-tuple-element.13, f32[]{:T(128)} %get-tuple-element.14), channel_id=1, replica_groups=mesh['cell_0'=8,'cell_1'=4,'sensor'=16] {'cell_1'}, use_global_device_ids=true, to_apply=%region_15.17 | all-reduce | flops 2 | bytes 16 | tf_op jit(solution)/shard_map/psum | solution.py:43
  (259 shorter events, 103.0 us)
Async XLA Ops:
  11.5 33.7 %all-to-all-start = ((f32[32,1,4096]{2,1,0:T(1,128)}), f32[32,1,4096]{2,1,0:T(1,128)S(1)}, u32[]{:S(2)}, u32[]{:S(2)}) async-start(f32[32,1,4096]{2,1,0:T(1,128)} %reshape.285), calls=%async_computation | async-start | bytes 1048576 | tf_op jit(solution)/shard_map/all_to_all | solution.py:33
  28.1 39.5 %collective-permute-start.1 = (f32[1,64,128]{1,2,0:T(8,128)S(1)}, f32[1,64,128]{1,2,0:T(8,128)S(1)}, u32[]{:S(2)}, u32[]{:S(2)}) collective-permute-start(f32[1,64,128]{1,2,0:T(8,128)S(1)} %get-tuple-element.44), channel_id=1, source_target_pairs={{16,0},{32,16},{48,32},{64,48},{80,64},{96,80},{112,96},{128,112},... | collective-permute-start | bytes 98312 | tf_op jit(solution)/shard_map/ppermute | solution.py:26
  29.4 38.2 %collective-permute-start = (f32[1,64,128]{1,2,0:T(8,128)S(1)}, f32[1,64,128]{1,2,0:T(8,128)S(1)}, u32[]{:S(2)}, u32[]{:S(2)}) collective-permute-start(f32[1,64,128]{1,2,0:T(8,128)S(1)} %get-tuple-element.43), channel_id=1, source_target_pairs={{0,16},{16,32},{32,48},{48,64},{64,80},{80,96},{96,112},{112,128},... | collective-permute-start | bytes 98312 | tf_op jit(solution)/shard_map/ppermute | solution.py:25
  59.1 35.1 %all-to-all-start.1 = ((f32[16,64,256]{2,1,0:T(8,128)}), f32[16,64,256]{2,1,0:T(8,128)S(1)}, u32[]{:S(2)}, u32[]{:S(2)}) async-start(f32[16,64,256]{2,1,0:T(8,128)} %broadcast_in_dim.52), calls=%async_computation.1 | async-start | bytes 2097152 | tf_op jit(solution)/shard_map/all_to_all | solution.py:33
  71.0 13.6 %collective-permute-start.3 = (f32[4,64,128]{1,2,0:T(8,128)S(1)}, f32[4,64,128]{1,2,0:T(8,128)S(1)}, u32[]{:S(2)}, u32[]{:S(2)}) collective-permute-start(f32[4,64,128]{1,2,0:T(8,128)S(1)} %get-tuple-element.38), channel_id=1, source_target_pairs={{16,0},{32,16},{48,32},{64,48},{80,64},{96,80},{112,96},{128,112},... | collective-permute-start | bytes 393224 | tf_op jit(solution)/shard_map/ppermute | solution.py:26
  72.3 12.5 %collective-permute-start.2 = (f32[4,64,128]{1,2,0:T(8,128)S(1)}, f32[4,64,128]{1,2,0:T(8,128)S(1)}, u32[]{:S(2)}, u32[]{:S(2)}) collective-permute-start(f32[4,64,128]{1,2,0:T(8,128)S(1)} %get-tuple-element.37), channel_id=1, source_target_pairs={{0,16},{16,32},{32,48},{48,64},{64,80},{80,96},{96,112},{112,128},... | collective-permute-start | bytes 393224 | tf_op jit(solution)/shard_map/ppermute | solution.py:25
  104.7 18.3 %collective-permute-start.5 = (f32[1,64,128]{1,2,0:T(8,128)S(1)}, f32[1,64,128]{1,2,0:T(8,128)S(1)}, u32[]{:S(2)}, u32[]{:S(2)}) collective-permute-start(f32[1,64,128]{1,2,0:T(8,128)S(1)} %get-tuple-element.42), channel_id=1, source_target_pairs={{16,0},{32,16},{48,32},{64,48},{80,64},{96,80},{112,96},{128,112},... | collective-permute-start | bytes 98312 | tf_op jit(solution)/shard_map/ppermute | solution.py:26
  106.0 17.0 %collective-permute-start.4 = (f32[1,64,128]{1,2,0:T(8,128)S(1)}, f32[1,64,128]{1,2,0:T(8,128)S(1)}, u32[]{:S(2)}, u32[]{:S(2)}) collective-permute-start(f32[1,64,128]{1,2,0:T(8,128)S(1)} %get-tuple-element.41), channel_id=1, source_target_pairs={{0,16},{16,32},{32,48},{48,64},{64,80},{80,96},{96,112},{112,128},... | collective-permute-start | bytes 98312 | tf_op jit(solution)/shard_map/ppermute | solution.py:25
  113.3 29.7 %all-to-all-start.2 = ((f32[32,1,4096]{2,1,0:T(1,128)}), f32[32,1,4096]{2,1,0:T(1,128)S(1)}, u32[]{:S(2)}, u32[]{:S(2)}) async-start(f32[32,1,4096]{2,1,0:T(1,128)} %reshape.287), calls=%async_computation.2 | async-start | bytes 1048576 | tf_op jit(solution)/shard_map/all_to_all | solution.py:33
  122.9 49.1 %copy-start.23 = (f32[64,64]{1,0:T(8,128)S(1)}, f32[64,64]{1,0:T(8,128)}, u32[]{:S(2)}) copy-start(f32[64,64]{1,0:T(8,128)} %copy-done.22) | copy-start | bytes 49156
  122.9 49.1 %copy-start.26 = (f32[64,64]{1,0:T(8,128)S(1)}, f32[64,64]{1,0:T(8,128)}, u32[]{:S(2)}) copy-start(f32[64,64]{1,0:T(8,128)} %param.10) | copy-start | bytes 49156
  126.0 64.9 %copy-start.1 = (f32[1,64,256]{1,2,0:T(8,128)}, f32[1,64,256]{1,2,0:T(8,128)S(1)}, u32[]{:S(2)}) copy-start(f32[1,64,256]{1,2,0:T(8,128)S(1)} %select_bitcast_fusion.4) | copy-start | bytes 196612
  126.2 64.8 %copy-start.3 = (f32[1,64,256]{1,2,0:T(8,128)}, f32[1,64,256]{1,2,0:T(8,128)S(1)}, u32[]{:S(2)}) copy-start(f32[1,64,256]{1,2,0:T(8,128)S(1)} %select_bitcast_fusion.5) | copy-start | bytes 196612
  126.3 64.7 %copy-start.5 = (f32[1,64,256]{1,2,0:T(8,128)}, f32[1,64,256]{1,2,0:T(8,128)S(1)}, u32[]{:S(2)}) copy-start(f32[1,64,256]{1,2,0:T(8,128)S(1)} %select_bitcast_fusion.6) | copy-start | bytes 196612
  126.4 64.6 %copy-start.7 = (f32[1,64,256]{1,2,0:T(8,128)}, f32[1,64,256]{1,2,0:T(8,128)S(1)}, u32[]{:S(2)}) copy-start(f32[1,64,256]{1,2,0:T(8,128)S(1)} %select_bitcast_fusion.7) | copy-start | bytes 196612
  147.3 22.2 %all-to-all-start.3 = ((f32[16,1,1]{2,1,0:T(1,128)}), f32[16,1,1]{2,1,0:T(1,128)S(1)}, u32[]{:S(2)}, u32[]{:S(2)}) async-start(f32[16,1,1]{2,1,0:T(1,128)} %broadcast_in_dim.55), calls=%async_computation.3 | async-start | bytes 16384 | tf_op jit(solution)/shard_map/all_to_all | solution.py:33
  183.1 34.6 %all-to-all-start.4 = ((f32[16,64,256]{2,1,0:T(8,128)}), f32[16,64,256]{2,1,0:T(8,128)S(1)}, u32[]{:S(2)}, u32[]{:S(2)}) async-start(f32[16,64,256]{2,1,0:T(8,128)} %broadcast_in_dim.95), calls=%async_computation.4 | async-start | bytes 2097152 | tf_op jit(solution)/shard_map/all_to_all | solution.py:33
  191.5 13.5 %collective-permute-start.7 = (f32[4,64,128]{1,2,0:T(8,128)S(1)}, f32[4,64,128]{1,2,0:T(8,128)S(1)}, u32[]{:S(2)}, u32[]{:S(2)}) collective-permute-start(f32[4,64,128]{1,2,0:T(8,128)S(1)} %get-tuple-element.36), channel_id=1, source_target_pairs={{16,0},{32,16},{48,32},{64,48},{80,64},{96,80},{112,96},{128,112},... | collective-permute-start | bytes 393224 | tf_op jit(solution)/shard_map/ppermute | solution.py:26
  192.8 15.6 %collective-permute-start.6 = (f32[4,64,128]{1,2,0:T(8,128)S(1)}, f32[4,64,128]{1,2,0:T(8,128)S(1)}, u32[]{:S(2)}, u32[]{:S(2)}) collective-permute-start(f32[4,64,128]{1,2,0:T(8,128)S(1)} %get-tuple-element.35), channel_id=1, source_target_pairs={{0,16},{16,32},{32,48},{48,64},{64,80},{80,96},{96,112},{112,128},... | collective-permute-start | bytes 393224 | tf_op jit(solution)/shard_map/ppermute | solution.py:25
  228.3 21.9 %collective-permute-start.9 = (f32[1,64,128]{1,2,0:T(8,128)S(1)}, f32[1,64,128]{1,2,0:T(8,128)S(1)}, u32[]{:S(2)}, u32[]{:S(2)}) collective-permute-start(f32[1,64,128]{1,2,0:T(8,128)S(1)} %get-tuple-element.40), channel_id=1, source_target_pairs={{16,0},{32,16},{48,32},{64,48},{80,64},{96,80},{112,96},{128,112},... | collective-permute-start | bytes 98312 | tf_op jit(solution)/shard_map/ppermute | solution.py:26
  229.6 20.6 %collective-permute-start.8 = (f32[1,64,128]{1,2,0:T(8,128)S(1)}, f32[1,64,128]{1,2,0:T(8,128)S(1)}, u32[]{:S(2)}, u32[]{:S(2)}) collective-permute-start(f32[1,64,128]{1,2,0:T(8,128)S(1)} %get-tuple-element.39), channel_id=1, source_target_pairs={{0,16},{16,32},{32,48},{48,64},{64,80},{80,96},{96,112},{112,128},... | collective-permute-start | bytes 98312 | tf_op jit(solution)/shard_map/ppermute | solution.py:25
  237.5 34.5 %all-to-all-start.5 = ((f32[32,1,4096]{2,1,0:T(1,128)}), f32[32,1,4096]{2,1,0:T(1,128)S(1)}, u32[]{:S(2)}, u32[]{:S(2)}) async-start(f32[32,1,4096]{2,1,0:T(1,128)} %reshape.289), calls=%async_computation.5 | async-start | bytes 1048576 | tf_op jit(solution)/shard_map/all_to_all | solution.py:33
  250.2 48.8 %copy-start.2 = (f32[1,64,256]{1,2,0:T(8,128)S(1)}, f32[1,64,256]{1,2,0:T(8,128)}, u32[]{:S(2)}) copy-start(f32[1,64,256]{1,2,0:T(8,128)} %copy-done.1) | copy-start | bytes 196612
  276.3 20.1 %all-to-all-start.6 = ((f32[16,1,1]{2,1,0:T(1,128)}), f32[16,1,1]{2,1,0:T(1,128)S(1)}, u32[]{:S(2)}, u32[]{:S(2)}) async-start(f32[16,1,1]{2,1,0:T(1,128)} %broadcast_in_dim.99), calls=%async_computation.6 | async-start | bytes 16384 | tf_op jit(solution)/shard_map/all_to_all | solution.py:33
  (40 other events, 951.5 us)
where the time goes:
time: 306 us; the launch traced here: 303 us
  starting transfers between devices  107 us (35%)
  blocking collectives  52.1 us (17%)
  matrix products  46.2 us (15%)
  waiting for transfers between devices  37.2 us (12%)
  local copies, waits for them, and re-layouts  33.8 us (11%)
  other arithmetic  20.9 us (7%)
  between operations  5.78 us (2%)
    all_to_all x7, starting transfers between devices, sent_to_all(): lax.all_to_all(jnp.broadcast_to(array[None], (devices, *array.shape)), ax...  75.7 us
    psum x4, blocking collectives, by_axis(): return functools.reduce(lax.psum, axes, array)  52.1 us
    ppermute x5, starting transfers between devices, padded_2(): before = lax.ppermute(last, axis, up)  25.3 us
    dot_general x12, matrix products, batched(): jnp.einsum('fsc,fc->fs', matrix, vector, preferred_element_type=jnp.float32)  20.8 us
    all_to_all x7, waiting for transfers between devices, sent_to_all(): lax.all_to_all(jnp.broadcast_to(array[None], (devices, *array.shape)), ax...  19.7 us
    dot_general x8, matrix products, transposed(): jnp.einsum('fsc,fs->fc', matrix, vector, preferred_element_type=jnp.float32)  16.1 us
    ppermute x5, waiting for transfers between devices, padded_2(): after = lax.ppermute(leading, axis, down)  14 us
    dot_general x20, matrix products, exact_dot(): jnp.dot(left, right, precision=lax.Precision.HIGHEST, preferred_element_t...  9.33 us
  transfers between devices with their start and end apart: 17, of which 7 were waited for; matrix products, arithmetic and copies ran while one was open for 14% of the time, Pallas kernels for 0%

commit v1 on v0

v1 whole, which is shorter than its diff:
```python
import functools

import jax
import jax.numpy as jnp
import numpy as np
from jax import lax
from jax.experimental import pallas as pl
from jax.experimental.pallas import tpu as pltpu
from jax.sharding import Mesh
from jax.sharding import PartitionSpec as P

NT = 64
NF = 65
ROW = 128
NY = 8
NZ = 4
NSEN = 16
ROWS = 144
SHRINK_SCALE = 0.4
TINY = 1e-06
F32 = jnp.float32
BF16 = jnp.bfloat16
MESH = pl.DeviceIdType.MESH
Y_ORDER = (4, 3, 5, 2, 6, 1, 7)
Z_ORDER = (2, 1, 3)


def high_low(table):
    high = table.astype(BF16)
    low = (table - high.astype(np.float32)).astype(BF16)
    return high, low


def tables():
    freq = np.arange(NF)[:, None]
    time = np.arange(NT)[None, :]
    phase = 2.0 * np.pi * (freq * time % (2 * NT)) / (2 * NT)
    cosine, sine = np.cos(phase), np.sin(phase)
    weight = np.where((freq == 0) | (freq == NF - 1), 1.0, 2.0) / (2 * NT)
    wcos, wsin = cosine * weight, sine * weight

    def interleaved(even, odd):
        out = np.zeros((ROWS, NT), np.float32)
        out[0 : 2 * NF : 2] = even
        out[1 : 2 * NF : 2] = odd
        return out

    analysis = interleaved(cosine, -sine)
    back = np.concatenate([interleaved(wcos, -wsin), interleaved(-wsin, -wcos)], axis=0)
    synthesis = np.concatenate([interleaved(wcos, -wsin).T, interleaved(wsin, wcos).T], axis=0)
    ah, al = high_low(analysis)
    bh, bl = high_low(back)
    sh, sl = high_low(synthesis)
    ch, cl = high_low(analysis.T)
    return (
        np.concatenate([ah, al, ah, al], axis=1),
        np.concatenate([bh, bl, bh, bl], axis=1),
        np.stack([sh, sl]),
        np.stack([ch, cl]),
    )


def split(value):
    high = value.astype(BF16)
    return high, (value - high.astype(F32)).astype(BF16)


def dot(left, right, dims=((1,), (0,))):
    return lax.dot_general(left, right, (dims, ((), ())), preferred_element_type=F32)


def dot3(table_ref, value):
    high, low = split(value)
    th = table_ref[0]
    return dot(th, high) + dot(th, low) + dot(table_ref[1], high)


def stacked(value):
    high, low = split(value)
    return jnp.concatenate([high, high, low, low], axis=0)


def body(
    k_hbm, obs_ref, x0_ref, m0_ref, nb_ref, tile_ref, w_ref, tf_ref, ta_ref, ti_ref, ts_ref,
    est_ref, aux_ref, mul_ref,
    kv, m_s, ab_s, l_s, q_s,
    send1, ya, zb, za, yb, mid_a, mid_b,
    sc_send, sc_mid, sy, sz, rs_send, rs_buf,
    gp, rs_in, g_s, b_s, dt_s, thr_s, h_n, h_s, gh_n, gh_s,
    jump_s, gj_s, mult_s,
    k_sem, h_ssem, h_rsem, ar_ssem, ar_rsem, sc_ssem, sc_rsem, rs_ssem, rs_rsem, gr_ssem, gr_rsem,
    gh_ssem, gh_rsem,
):
    my = lax.axis_index("y")
    mz = lax.axis_index("zh")
    ms = lax.axis_index("sensor")
    cell = my * NZ + mz
    nxt = (cell + 1) % (NY * NZ)
    prv = (cell + NY * NZ - 1) % (NY * NZ)
    nxt_id = {"y": nxt // NZ, "zh": nxt % NZ}
    prv_id = {"y": prv // NZ, "zh": prv % NZ}
    y_ids = [{"y": (my + j) % NY} for j in Y_ORDER]
    z_ids = [{"zh": (mz + j) % NZ} for j in Z_ORDER]
    s_nums = [(ms + j) % NSEN for j in (7, 9, 6, 10, 5, 11, 4, 12, 3, 13, 8, 2, 14, 1, 15)]

    barrier = pltpu.get_barrier_semaphore()
    everyone = y_ids + z_ids + [{"sensor": p} for p in s_nums] + [nxt_id, prv_id]
    for who in everyone:
        pl.semaphore_signal(barrier, inc=1, device_id=who, device_id_type=MESH)

    bounds = (0, 16, 32, 48, 65)

    def k_copy(plane, q):
        lo, hi = bounds[q], bounds[q + 1]
        return pltpu.make_async_copy(
            k_hbm.at[plane, pl.ds(lo, hi - lo)],
            kv.at[pl.ds(lo, hi - lo), pl.ds(64 * plane, 64)],
            k_sem.at[plane, q],
        )

    for q in range(4):
        for plane in range(2):
            k_copy(plane, q).start()

    def send(src, dst, who, ssem, rsem):
        pltpu.make_async_remote_copy(
            src_ref=src, dst_ref=dst, send_sem=ssem, recv_sem=rsem, device_id=who,
            device_id_type=MESH,
        ).start()

    def wait_for(view, sem):
        pltpu.make_async_copy(view, view, sem).wait()

    lane = lax.broadcasted_iota(jnp.int32, (1, ROW), 1)
    left_half = lane < 64

    column = jnp.sum(
        jnp.where(
            lax.broadcasted_iota(jnp.int32, (64, 64), 0)
            == lax.broadcasted_iota(jnp.int32, (64, 64), 1),
            jnp.broadcast_to(w_ref[...], (64, 64)), 0.0,
        ),
        axis=1, keepdims=True,
    )
    labels = lax.broadcasted_iota(jnp.int32, (64, 2 * ROW), 0)
    threshold = SHRINK_SCALE * jnp.sum(
        jnp.where(labels == tile_ref[...], column, 0.0), axis=0, keepdims=True
    )
    thr_s[0] = jnp.broadcast_to(threshold[:, :ROW], (8, ROW))
    thr_s[1] = jnp.broadcast_to(threshold[:, ROW:], (8, ROW))
    own = cell * (2 * ROW) + lax.broadcasted_iota(jnp.int32, (1, 2 * ROW), 1)
    linked = [[None, None] for _ in range(4)]
    for k in range(4):
        both = jnp.where(nb_ref[pl.ds(k, 1), :] != own, 1.0, 0.0)
        linked[k][0] = both[:, :ROW] > 0.5
        linked[k][1] = both[:, ROW:] > 0.5

    group_row = lax.broadcasted_iota(jnp.int32, (8, ROW), 0) // 2

    def forward(field, first):
        m_s[...] = dot(tf_ref[...], stacked(field))

        def step(i, carry):
            moved = m_s[pl.ds(pl.multiple_of(8 * i, 8), 8), :].astype(BF16)
            weights = kv[pl.ds(4 * i, 4)].reshape(512, 256)
            out = dot(moved, weights, ((1,), (1,)))
            kept = out[:, 0:ROW]
            for j in range(1, 4):
                kept = jnp.where(group_row == j, out[:, j * ROW : (j + 1) * ROW], kept)
            ab_s[pl.ds(pl.multiple_of(8 * i, 8), 8), :] = kept
            return carry

        if first:
            for q in range(4):
                k_copy(0, q).wait()
                k_copy(1, q).wait()
                lax.fori_loop(4 * q, 4 * q + 4, step, 0, unroll=2)
        else:
            lax.fori_loop(0, 16, step, 0, unroll=2)
        tail = m_s[128:136, :].astype(BF16)
        ab_s[128:136, :] = dot(tail, kv[64], ((1,), (1,)))
        ab_s[136:144, :] = jnp.zeros((8, ROW), F32)
        out = dot3(ti_ref, ab_s[...])
        low = out[0:32] - pltpu.roll(out[64:96], 64, 1)
        high = pltpu.roll(out[32:64], 64, 1) - out[96:128]
        return jnp.where(left_half, low, high)

    def adjoint(packed, dst):
        turned = pltpu.roll(packed, 64, 1)
        doubled = jnp.concatenate(
            [jnp.where(left_half, packed, turned), jnp.where(left_half, turned, packed)], axis=0
        )
        out = dot(ta_ref[...], stacked(doubled))
        l_s[...] = jnp.where(left_half, out[:ROWS], out[ROWS:])

        def step(i, carry):
            rows = l_s[pl.ds(pl.multiple_of(8 * i, 8), 8), :]
            moved = jnp.concatenate(
                [jnp.where(group_row == j, rows, 0.0) for j in range(4)], axis=1
            ).astype(BF16)
            weights = kv[pl.ds(4 * i, 4)].reshape(512, 256)
            q_s[pl.ds(pl.multiple_of(8 * i, 8), 8), :] = dot(moved, weights)
            return carry

        lax.fori_loop(0, 16, step, 0, unroll=2)
        q_s[128:136, :] = dot(l_s[128:136, :].astype(BF16), kv[64])
        q_s[136:144, :] = jnp.zeros((8, 256), F32)
        out = dot3(ts_ref, q_s[...])
        dst[0:8] = out[:, :ROW].reshape(8, 8, ROW)
        dst[8:16] = out[:, ROW:].reshape(8, 8, ROW)

    def sum_start(n, packed):
        send1[n] = packed
        ya[n, my] = packed[0:16]
        zb[n, mz] = packed[16:32]
        for who in y_ids:
            send(send1.at[n, pl.ds(0, 16)], ya.at[n, my], who, ar_ssem.at[n, 0], ar_rsem.at[n, 0])
        for who in z_ids:
            send(send1.at[n, pl.ds(16, 16)], zb.at[n, mz], who, ar_ssem.at[n, 1], ar_rsem.at[n, 1])

    def sum_middle(n):
        wait_for(zb.at[n, pl.ds(0, NZ - 1)], ar_rsem.at[n, 1])
        part = jnp.sum(zb[n], axis=0)
        mid_b[n] = part
        yb[n, my] = part
        for who in y_ids:
            send(mid_b.at[n], yb.at[n, my], who, ar_ssem.at[n, 2], ar_rsem.at[n, 2])
        wait_for(ya.at[n, pl.ds(0, NY - 1)], ar_rsem.at[n, 0])
        part = jnp.sum(ya[n], axis=0)
        mid_a[n] = part
        za[n, mz] = part
        for who in z_ids:
            send(mid_a.at[n], za.at[n, mz], who, ar_ssem.at[n, 3], ar_rsem.at[n, 3])

    def sum_end(n):
        wait_for(za.at[n, pl.ds(0, NZ - 1)], ar_rsem.at[n, 3])
        wait_for(yb.at[n, pl.ds(0, NY - 1)], ar_rsem.at[n, 2])
        return jnp.concatenate([jnp.sum(za[n], axis=0), jnp.sum(yb[n], axis=0)], axis=0)

    def scalars_start(n, one, two):
        sc_send[n, pl.ds(0, 1), :] = one
        sc_send[n, pl.ds(1, 1), :] = two
        sy[n, my, pl.ds(0, 1), :] = one
        sy[n, my, pl.ds(1, 1), :] = two
        for who in y_ids:
            send(sc_send.at[n], sy.at[n, my], who, sc_ssem.at[n, 0], sc_rsem.at[n, 0])

    def scalars_middle(n):
        wait_for(sy.at[n, pl.ds(0, NY - 1)], sc_rsem.at[n, 0])
        part = jnp.sum(sy[n], axis=0)
        sc_mid[n] = part
        sz[n, mz] = part
        for who in z_ids:
            send(sc_mid.at[n], sz.at[n, mz], who, sc_ssem.at[n, 1], sc_rsem.at[n, 1])

    def response_start(n, packed):
        row = jnp.sum(packed * packed, axis=0, keepdims=True)
        rs_send[n] = row
        rs_buf[n, ms] = row
        for p in s_nums:
            send(rs_send.at[n], rs_buf.at[n, ms], {"sensor": p}, rs_ssem.at[n], rs_rsem.at[n])

    def step_size(n):
        wait_for(sz.at[n, pl.ds(0, NZ - 1)], sc_rsem.at[n, 1])
        wait_for(rs_buf.at[n, pl.ds(0, NSEN - 1)], rs_rsem.at[n])
        sums = jnp.sum(sz[n], axis=0)
        total = jnp.sum(sums, axis=1, keepdims=True)
        response = jnp.sum(jnp.sum(rs_buf[n], axis=0), axis=1, keepdims=True)
        return total[0:1] / (response + total[1:2] + TINY)

    def scatter_start(n):
        rs_in[n, ms] = gp[n, ms]
        for p in s_nums:
            send(gp.at[n, p], rs_in.at[n, ms], {"sensor": p}, gr_ssem.at[n, 0], gr_rsem.at[n, 0])

    def scatter_end(n):
        wait_for(rs_in.at[n, pl.ds(0, NSEN - 1)], gr_rsem.at[n, 0])
        return jnp.sum(rs_in[n], axis=0)

    def gather(n, piece):
        b_s[1 + n] = piece
        g_s[n, ms] = piece
        for p in s_nums:
            send(b_s.at[1 + n], g_s.at[n, ms], {"sensor": p}, gr_ssem.at[n, 1], gr_rsem.at[n, 1])
        wait_for(g_s.at[n, pl.ds(0, NSEN - 1)], gr_rsem.at[n, 1])
        send(g_s.at[n, pl.ds(8, 8)], gh_n.at[n], nxt_id, gh_ssem.at[n, 0], gh_rsem.at[n, 0])
        send(g_s.at[n, pl.ds(0, 8)], gh_s.at[n], prv_id, gh_ssem.at[n, 1], gh_rsem.at[n, 1])
        return g_s[n, 0:8].reshape(NT, ROW), g_s[n, 8:16].reshape(NT, ROW)

    def halo(n):
        wait_for(gh_n.at[n], gh_rsem.at[n, 0])
        wait_for(gh_s.at[n], gh_rsem.at[n, 1])
        return gh_n[n].reshape(NT, ROW), gh_s[n].reshape(NT, ROW)

    def jumps(dst, above, first, second, below):
        rows = (first, second)
        for r in range(2):
            dst[r] = jnp.where(linked[0][r], pltpu.roll(rows[r], ROW - 1, 1) - rows[r], 0.0)
            dst[2 + r] = jnp.where(linked[1][r], pltpu.roll(rows[r], 1, 1) - rows[r], 0.0)
            north = above if r == 0 else first
            south = second if r == 0 else below
            dst[4 + r] = jnp.where(linked[2][r], north - rows[r], 0.0)
            dst[6 + r] = jnp.where(linked[3][r], south - rows[r], 0.0)

    def squares(refs):
        total = jnp.zeros((1, ROW), F32)
        for value in refs:
            total = total + jnp.sum(value * value, axis=0, keepdims=True)
        return total

    def divergence(v):
        for r in range(2):
            from_south = v[5] if r == 0 else v[9]
            from_north = v[8] if r == 0 else v[6]
            total = jnp.where(linked[1][r], pltpu.roll(v[r], 1, 1), 0.0)
            total = total + jnp.where(linked[0][r], pltpu.roll(v[2 + r], ROW - 1, 1), 0.0)
            total = total + jnp.where(linked[3][r], from_south, 0.0)
            total = total + jnp.where(linked[2][r], from_north, 0.0)
            for k in range(4):
                total = total - jnp.where(linked[k][r], v[2 * k + r], 0.0)
            dt_s[8 * r : 8 * r + 8] = total.reshape(8, 8, ROW)

    first_sum = forward(x0_ref[...], True)
    pl.semaphore_wait(barrier, len(everyone))
    sum_start(0, first_sum)
    send(x0_ref.at[:, pl.ds(ROW, ROW)], h_n.at[pl.ds(0, 64)], nxt_id, h_ssem.at[0], h_rsem.at[0])
    send(m0_ref.at[3, :, pl.ds(ROW, ROW)], h_n.at[pl.ds(64, 64)], nxt_id, h_ssem.at[0], h_rsem.at[0])
    send(thr_s.at[1], h_n.at[pl.ds(128, 8)], nxt_id, h_ssem.at[0], h_rsem.at[0])
    send(x0_ref.at[:, pl.ds(0, ROW)], h_s.at[pl.ds(0, 64)], prv_id, h_ssem.at[1], h_rsem.at[1])
    send(m0_ref.at[2, :, pl.ds(0, ROW)], h_s.at[pl.ds(64, 64)], prv_id, h_ssem.at[1], h_rsem.at[1])
    send(thr_s.at[0], h_s.at[pl.ds(128, 8)], prv_id, h_ssem.at[1], h_rsem.at[1])
    sum_middle(0)
    wait_for(h_n, h_rsem.at[0])
    wait_for(h_s, h_rsem.at[1])
    start = [m0_ref[k, :, r * ROW : (r + 1) * ROW] for k in range(4) for r in range(2)]
    start = start + [h_n[64:128], h_s[64:128]]
    divergence(start)
    jumps(jump_s, h_n[0:64], x0_ref[:, 0:ROW], x0_ref[:, ROW:], h_s[0:64])
    observed = jnp.concatenate([obs_ref[0:32], obs_ref[32:64]], axis=1)
    misfit = sum_end(0) - observed

    adjoint(misfit, gp.at[0])
    scatter_start(0)
    piece = scatter_end(0)
    b_s[0] = piece
    grad_a, grad_b = gather(0, piece + dt_s[ms])
    part = forward(jnp.concatenate([grad_a, grad_b], axis=1), False)
    sum_start(1, part)
    above, below = halo(0)
    grad_a = g_s[0, 0:8].reshape(NT, ROW)
    grad_b = g_s[0, 8:16].reshape(NT, ROW)
    jumps(gj_s, above, grad_a, grad_b, below)
    scalars_start(0, squares([grad_a, grad_b]), squares([gj_s[i] for i in range(8)]))
    sum_middle(1)
    scalars_middle(0)
    response = sum_end(1)
    response_start(0, response)
    adjoint(response, gp.at[1])
    scatter_start(1)
    size = step_size(0)
    penalty = []
    thresholds = [thr_s[0, 0:1], thr_s[1, 0:1], h_n[128:129], h_s[128:129]]
    for i in range(10):
        if i < 8:
            moved = jump_s[i] - size * gj_s[i]
            limit = thresholds[i % 2]
            held = m0_ref[i // 2, :, (i % 2) * ROW : (i % 2 + 1) * ROW]
            jump_s[i] = moved
        else:
            source = 4 if i == 8 else 7
            moved = -jump_s[source]
            limit = thresholds[i - 6]
            held = h_n[64:128] if i == 8 else h_s[64:128]
        shifted = moved + held
        shrunk = jnp.maximum(shifted - limit, 0.0) - jnp.maximum(-shifted - limit, 0.0)
        rest = shifted - shrunk
        if i < 8:
            mult_s[i] = rest
        penalty.append(moved - shrunk + rest)
    divergence(penalty)
    est_ref[:, 0:ROW] = x0_ref[:, 0:ROW] - size * g_s[0, 0:8].reshape(NT, ROW)
    est_ref[:, ROW:] = x0_ref[:, ROW:] - size * g_s[0, 8:16].reshape(NT, ROW)

    piece = b_s[0] - size * scatter_end(1)
    grad_a, grad_b = gather(1, piece + dt_s[ms])
    part = forward(jnp.concatenate([grad_a, grad_b], axis=1), False)
    sum_start(2, part)
    above, below = halo(1)
    grad_a = g_s[1, 0:8].reshape(NT, ROW)
    grad_b = g_s[1, 8:16].reshape(NT, ROW)
    jumps(gj_s, above, grad_a, grad_b, below)
    scalars_start(1, squares([grad_a, grad_b]), squares([gj_s[i] for i in range(8)]))
    sum_middle(2)
    scalars_middle(1)
    response_start(1, sum_end(2))
    size = step_size(1)
    est_ref[:, 0:ROW] = est_ref[:, 0:ROW] - size * g_s[1, 0:8].reshape(NT, ROW)
    est_ref[:, ROW:] = est_ref[:, ROW:] - size * g_s[1, 8:16].reshape(NT, ROW)
    for i in range(8):
        shifted = jump_s[i] - size * gj_s[i] + mult_s[i]
        limit = thresholds[i % 2]
        shrunk = jnp.maximum(shifted - limit, 0.0) - jnp.maximum(-shifted - limit, 0.0)
        k, r = i // 2, i % 2
        aux_ref[k, :, r * ROW : (r + 1) * ROW] = shrunk
        mul_ref[k, :, r * ROW : (r + 1) * ROW] = shifted - shrunk

    wait_for(h_n, h_ssem.at[0])
    wait_for(h_s, h_ssem.at[1])
    for n in range(3):
        wait_for(ya.at[n, pl.ds(0, NY - 1)], ar_ssem.at[n, 0])
        wait_for(zb.at[n, pl.ds(0, NZ - 1)], ar_ssem.at[n, 1])
        wait_for(yb.at[n, pl.ds(0, NY - 1)], ar_ssem.at[n, 2])
        wait_for(za.at[n, pl.ds(0, NZ - 1)], ar_ssem.at[n, 3])
    for n in range(2):
        wait_for(sy.at[n, pl.ds(0, NY - 1)], sc_ssem.at[n, 0])
        wait_for(sz.at[n, pl.ds(0, NZ - 1)], sc_ssem.at[n, 1])
        wait_for(rs_buf.at[n, pl.ds(0, NSEN - 1)], rs_ssem.at[n])
        wait_for(rs_in.at[n, pl.ds(0, NSEN - 1)], gr_ssem.at[n, 0])
        wait_for(g_s.at[n, pl.ds(0, NSEN - 1)], gr_ssem.at[n, 1])
        wait_for(gh_n.at[n], gh_ssem.at[n, 0])
        wait_for(gh_s.at[n], gh_ssem.at[n, 1])


def per_device(kernel, observed, start_model, start_multiplier, neighbours, tile, weight):
    vmem = pl.BlockSpec(memory_space=pltpu.VMEM)
    scratch = lambda *shape, dtype=F32: pltpu.VMEM(shape, dtype)
    dma = lambda *shape: pltpu.SemaphoreType.DMA(shape)
    analysis, back, synthesis, closing = (jnp.asarray(t) for t in tables())
    return pl.pallas_call(
        body,
        out_shape=(
            jax.ShapeDtypeStruct((NT, 256), F32),
            jax.ShapeDtypeStruct((4, NT, 256), F32),
            jax.ShapeDtypeStruct((4, NT, 256), F32),
        ),
        in_specs=[pl.BlockSpec(memory_space=pl.ANY)] + [vmem] * 10,
        out_specs=(vmem, vmem, vmem),
        scratch_shapes=[
            scratch(NF, 128, 256, dtype=BF16),
            scratch(ROWS, 256),
            scratch(ROWS, ROW),
            scratch(ROWS, ROW),
            scratch(ROWS, 256),
            scratch(3, 32, ROW),
            scratch(3, NY, 16, ROW),
            scratch(3, NZ, 16, ROW),
            scratch(3, NZ, 16, ROW),
            scratch(3, NY, 16, ROW),
            scratch(3, 16, ROW),
            scratch(3, 16, ROW),
            scratch(2, 2, ROW),
            scratch(2, 2, ROW),
            scratch(2, NY, 2, ROW),
            scratch(2, NZ, 2, ROW),
            scratch(2, 1, ROW),
            scratch(2, NSEN, 1, ROW),
            scratch(2, 16, 8, ROW),
            scratch(2, NSEN, 8, ROW),
            scratch(2, 16, 8, ROW),
            scratch(3, 8, ROW),
            scratch(16, 8, ROW),
            scratch(2, 8, ROW),
            scratch(136, ROW),
            scratch(136, ROW),
            scratch(2, 8, 8, ROW),
            scratch(2, 8, 8, ROW),
            scratch(8, NT, ROW),
            scratch(8, NT, ROW),
            scratch(8, NT, ROW),
            dma(2, 4),
            dma(2),
            dma(2),
            dma(3, 4),
            dma(3, 4),
            dma(2, 2),
            dma(2, 2),
            dma(2),
            dma(2),
            dma(2, 2),
            dma(2, 2),
            dma(2, 2),
            dma(2, 2),
        ],
        compiler_params=pltpu.CompilerParams(
            collective_id=0, has_side_effects=True, vmem_limit_bytes=48 * 1024 * 1024
        ),
        name="inversion",
    )(
        kernel, observed, start_model, start_multiplier, neighbours, tile.reshape(1, 256),
        weight.reshape(1, 64), analysis, back, synthesis, closing,
    )


def solution(mesh):
    split_mesh = Mesh(mesh.devices.reshape(NY, NZ, NSEN), ("y", "zh", "sensor"))
    cells = ("y", "zh")
    in_specs = (
        P(None, None, "sensor", cells),
        P(None, "sensor"),
        P(None, cells),
        P(None, None, cells),
        P(None, cells),
        P(cells),
        P(),
    )
    out_specs = (P(None, cells), P(None, None, cells), P(None, None, cells))
    return jax.shard_map(
        per_device, mesh=split_mesh, in_specs=in_specs, out_specs=out_specs, check_vma=False
    )
```

time: 306 us -> 89.5 us (0.29)
  starting transfers between devices: 107 us -> 0 us
  Pallas kernels: 0 us -> 76 us
  blocking collectives: 52.1 us -> 0 us
  matrix products: 46.2 us -> 0 us
  waiting for transfers between devices: 37.2 us -> 0 us
  local copies, waits for them, and re-layouts: 33.8 us -> 12.3 us
  other arithmetic: 20.9 us -> 0 us
  between operations: 5.78 us -> 0.66 us
    pallas_call x0 -> x1, Pallas kernels: none -> 76 us  [per_device(): pl.pallas_call(body, out_shape=(jax.ShapeDtypeStruct((NT, 256), F32), jax...]
    all_to_all x7 -> x0, starting transfers between devices: 75.7 us -> none  [sent_to_all(): lax.all_to_all(jnp.broadcast_to(array[None], (devices, *array.shape)), ax...]
    psum x4 -> x0, blocking collectives: 52.1 us -> none  [by_axis(): return functools.reduce(lax.psum, axes, array)]
    dot_general x40 -> x0, matrix products: 46.2 us -> none  [the longest x12 20.8 us: batched(): jnp.einsum('fsc,fc->fs', matrix, vector, preferred_element_type=jnp.float32)]
    ppermute x10 -> x0, starting transfers between devices: 31.7 us -> none  [the longest x5 25.3 us: padded_2(): before = lax.ppermute(last, axis, up)]
    all_to_all x7 -> x0, waiting for transfers between devices: 19.7 us -> none  [sent_to_all(): lax.all_to_all(jnp.broadcast_to(array[None], (devices, *array.shape)), ax...]
    ppermute x10 -> x0, waiting for transfers between devices: 17.5 us -> none  [the longest x5 14 us: padded_2(): after = lax.ppermute(leading, axis, down)]
    gather x20 -> x0, local copies, waits for them, and re-layouts: 17.3 us -> none  [the longest x12 8.73 us: differences(): jnp.take(extended[0], local_index[direction], axis=1)]
  transfers between devices with their start and end apart: 17 -> 0, of which waited for: 7 -> 0; matrix products, arithmetic and copies ran while one was open for 14% -> 0% of each run, Pallas kernels for 0% -> 0%
where the time goes in v1:
time: 89.5 us; the launch traced here: 89 us
  Pallas kernels  76 us (85%)
  local copies, waits for them, and re-layouts  12.3 us (14%)
    pallas_call x1, Pallas kernels, per_device(): pl.pallas_call(body, out_shape=(jax.ShapeDtypeStruct((NT, 256), F32), jax...  76 us
    unnamed x25, local copies, waits for them, and re-layouts  12.3 us

profile of v1, /device:TPU:1, one launch (start us, length us, event | category | flops | bytes accessed | tf_op | source)
XLA Modules:
  0.0 89.0 jit_solution(2688612279059985217)
XLA Ops:
  0.6 0.0 copy-start
  0.6 2.2 %copy-done = bf16[2,65,64,256]{3,2,1,0:T(8,128)(2,1)S(1)} copy-done((bf16[2,65,64,256]{3,2,1,0:T(8,128)(2,1)S(1)}, bf16[2,65,64,256]{3,2,1,0:T(8,128)(2,1)}, u32[]{:S(2)}) %copy-start) | copy-done | bytes 4259864
  2.8 0.9 %copy-done.1 = f32[4,64,256]{2,1,0:T(8,128)S(1)} copy-done((f32[4,64,256]{2,1,0:T(8,128)S(1)}, f32[4,64,256]{2,1,0:T(8,128)}, u32[]{:S(2)}) %copy-start.1) | copy-done | bytes 262168
  3.8 0.0 copy-start.2
  3.8 0.9 %copy-done.2 = bf16[288,256]{1,0:T(8,128)(2,1)S(1)} copy-done((bf16[288,256]{1,0:T(8,128)(2,1)S(1)}, bf16[288,256]{1,0:T(8,128)(2,1)}, u32[]{:S(2)}) %copy-start.2) | copy-done | bytes 147480
  4.7 0.0 copy-start.3
  4.7 0.9 %copy-done.3 = bf16[2,128,144]{2,1,0:T(8,128)(2,1)S(1)} copy-done((bf16[2,128,144]{2,1,0:T(8,128)(2,1)S(1)}, bf16[2,128,144]{2,1,0:T(8,128)(2,1)}, u32[]{:S(2)}) %copy-start.3) | copy-done | bytes 73752
  5.6 0.0 copy-start.4
  5.6 0.9 copy-done.4
  6.5 0.0 copy-start.5
  6.5 0.8 copy-done.5
  7.3 0.0 copy-start.6
  7.3 0.8 copy-done.6
  8.2 0.0 copy-start.7
  8.2 0.8 copy-done.7
  8.9 0.0 copy-start.8
  8.9 0.7 copy-done.8
  9.6 0.0 copy-start.9
  9.6 0.7 copy-done.9
  10.3 0.7 copy-done.10
  11.0 76.0 %inversion.1 = (f32[64,256]{1,0:T(8,128)S(1)}, f32[4,64,256]{2,1,0:T(8,128)S(1)}, f32[4,64,256]{2,1,0:T(8,128)S(1)}) custom-call(bf16[2,65,64,256]{3,2,1,0:T(8,128)(2,1)S(1)} %copy-done, f32[64,64]{1,0:T(8,128)S(1)} %copy-done.7, f32[64,256]{1,0:T(8,128)S(1)} %copy-done.5, f32[4,64,256]{2,1,0:T(8,128)S(1)} %copy-done.1, s32[4,256]{1,0:T(4,128)S(1)} %copy-done.8, ...), custom_call_target="tpu_custom_call" | custom-call | tf_op jit(solution)/shard_map/inversion/pallas_call | solution.py:429
  87.0 0.6 copy.17
  87.6 0.7 copy.18
  88.3 0.7 copy.19
  (2 shorter events, 0.0 us)
Async XLA Ops:
  0.6 2.2 %copy-start = (bf16[2,65,64,256]{3,2,1,0:T(8,128)(2,1)S(1)}, bf16[2,65,64,256]{3,2,1,0:T(8,128)(2,1)}, u32[]{:S(2)}) copy-start(bf16[2,65,64,256]{3,2,1,0:T(8,128)(2,1)} %k_hbm.1) | copy-start | bytes 12779524
  2.8 0.9 %copy-start.1 = (f32[4,64,256]{2,1,0:T(8,128)S(1)}, f32[4,64,256]{2,1,0:T(8,128)}, u32[]{:S(2)}) copy-start(f32[4,64,256]{2,1,0:T(8,128)} %m0_ref.1) | copy-start | bytes 786436
  3.8 0.9 %copy-start.2 = (bf16[288,256]{1,0:T(8,128)(2,1)S(1)}, bf16[288,256]{1,0:T(8,128)(2,1)}, u32[]{:S(2)}) copy-start(bf16[288,256]{1,0:T(8,128)(2,1)} %constant.9.clone.ta_ref) | copy-start | bytes 442372
  4.7 0.9 %copy-start.3 = (bf16[2,128,144]{2,1,0:T(8,128)(2,1)S(1)}, bf16[2,128,144]{2,1,0:T(8,128)(2,1)}, u32[]{:S(2)}) copy-start(bf16[2,128,144]{2,1,0:T(8,128)(2,1)} %constant.10.clone.ti_ref) | copy-start | bytes 221188
  5.6 0.9 copy-start.4
  6.5 0.8 copy-start.5
  7.3 0.8 copy-start.6
  8.2 0.8 copy-start.7
  8.9 0.7 copy-start.8
  9.6 0.7 copy-start.9
  10.3 0.7 copy-start.10

commit v2 on v1

--- a/solution.py
+++ b/solution.py
@@ -18,6 +18,8 @@
 ROWS = 144
 SHRINK_SCALE = 0.4
 TINY = 1e-06
+UNROLL = 16
+MAIN_VMEM = 67043328
 F32 = jnp.float32
 BF16 = jnp.bfloat16
 MESH = pl.DeviceIdType.MESH
@@ -81,14 +83,14 @@
 
 
 def body(
-    k_hbm, obs_ref, x0_ref, m0_ref, nb_ref, tile_ref, w_ref, tf_ref, ta_ref, ti_ref, ts_ref,
-    est_ref, aux_ref, mul_ref,
-    kv, m_s, ab_s, l_s, q_s,
+    k_hbm, obs_hbm, x0_hbm, m0_hbm, nb_hbm, tile_hbm, w_hbm, tf_hbm, ta_hbm, ti_hbm, ts_hbm,
+    est_hbm, aux_hbm, mul_hbm,
+    kv, est_ref, aux_ref, mul_ref, obs_ref, x0_ref, m0_ref, nb_ref, tile_ref, w_ref, tf_ref, ta_ref, ti_ref, ts_ref, m_s, ab_s, l_s, q_s,
     send1, ya, zb, za, yb, mid_a, mid_b,
     sc_send, sc_mid, sy, sz, rs_send, rs_buf,
     gp, rs_in, g_s, b_s, dt_s, thr_s, h_n, h_s, gh_n, gh_s,
     jump_s, gj_s, mult_s,
-    k_sem, h_ssem, h_rsem, ar_ssem, ar_rsem, sc_ssem, sc_rsem, rs_ssem, rs_rsem, gr_ssem, gr_rsem,
+    k_sem, in_sem, out_sem, h_ssem, h_rsem, ar_ssem, ar_rsem, sc_ssem, sc_rsem, rs_ssem, rs_rsem, gr_ssem, gr_rsem,
     gh_ssem, gh_rsem,
 ):
     my = lax.axis_index("y")
@@ -103,6 +105,17 @@
     z_ids = [{"zh": (mz + j) % NZ} for j in Z_ORDER]
     s_nums = [(ms + j) % NSEN for j in (7, 9, 6, 10, 5, 11, 4, 12, 3, 13, 8, 2, 14, 1, 15)]
 
+    def load(i):
+        src, dst = loads[i]
+        return pltpu.make_async_copy(src, dst, in_sem.at[i])
+
+    loads = (
+        (x0_hbm, x0_ref), (tf_hbm, tf_ref), (ti_hbm, ti_ref), (w_hbm, w_ref), (tile_hbm, tile_ref),
+        (nb_hbm, nb_ref), (m0_hbm, m0_ref), (obs_hbm, obs_ref), (ta_hbm, ta_ref), (ts_hbm, ts_ref),
+    )
+    load(0).start()
+    load(1).start()
+
     barrier = pltpu.get_barrier_semaphore()
     everyone = y_ids + z_ids + [{"sensor": p} for p in s_nums] + [nxt_id, prv_id]
     for who in everyone:
@@ -121,6 +134,8 @@
     for q in range(4):
         for plane in range(2):
             k_copy(plane, q).start()
+    for i in range(2, 10):
+        load(i).start()
 
     def send(src, dst, who, ssem, rsem):
         pltpu.make_async_remote_copy(
@@ -134,26 +149,23 @@
     lane = lax.broadcasted_iota(jnp.int32, (1, ROW), 1)
     left_half = lane < 64
 
-    column = jnp.sum(
-        jnp.where(
-            lax.broadcasted_iota(jnp.int32, (64, 64), 0)
-            == lax.broadcasted_iota(jnp.int32, (64, 64), 1),
-            jnp.broadcast_to(w_ref[...], (64, 64)), 0.0,
-        ),
-        axis=1, keepdims=True,
-    )
-    labels = lax.broadcasted_iota(jnp.int32, (64, 2 * ROW), 0)
-    threshold = SHRINK_SCALE * jnp.sum(
-        jnp.where(labels == tile_ref[...], column, 0.0), axis=0, keepdims=True
-    )
-    thr_s[0] = jnp.broadcast_to(threshold[:, :ROW], (8, ROW))
-    thr_s[1] = jnp.broadcast_to(threshold[:, ROW:], (8, ROW))
-    own = cell * (2 * ROW) + lax.broadcasted_iota(jnp.int32, (1, 2 * ROW), 1)
-    linked = [[None, None] for _ in range(4)]
-    for k in range(4):
-        both = jnp.where(nb_ref[pl.ds(k, 1), :] != own, 1.0, 0.0)
-        linked[k][0] = both[:, :ROW] > 0.5
-        linked[k][1] = both[:, ROW:] > 0.5
+    def prepare():
+        for i in (3, 4, 5):
+            load(i).wait()
+        column = jnp.sum(
+            jnp.where(
+                lax.broadcasted_iota(jnp.int32, (64, 64), 0)
+                == lax.broadcasted_iota(jnp.int32, (64, 64), 1),
+                jnp.broadcast_to(w_ref[...], (64, 64)), 0.0,
+            ),
+            axis=1, keepdims=True,
+        )
+        labels = lax.broadcasted_iota(jnp.int32, (64, 2 * ROW), 0)
+        threshold = SHRINK_SCALE * jnp.sum(
+            jnp.where(labels == tile_ref[...], column, 0.0), axis=0, keepdims=True
+        )
+        thr_s[0] = jnp.broadcast_to(threshold[:, :ROW], (8, ROW))
+        thr_s[1] = jnp.broadcast_to(threshold[:, ROW:], (8, ROW))
 
     group_row = lax.broadcasted_iota(jnp.int32, (8, ROW), 0) // 2
 
@@ -174,12 +186,14 @@
             for q in range(4):
                 k_copy(0, q).wait()
                 k_copy(1, q).wait()
-                lax.fori_loop(4 * q, 4 * q + 4, step, 0, unroll=2)
+                lax.fori_loop(4 * q, 4 * q + 4, step, 0, unroll=4)
         else:
-            lax.fori_loop(0, 16, step, 0, unroll=2)
+            lax.fori_loop(0, 16, step, 0, unroll=UNROLL)
         tail = m_s[128:136, :].astype(BF16)
         ab_s[128:136, :] = dot(tail, kv[64], ((1,), (1,)))
         ab_s[136:144, :] = jnp.zeros((8, ROW), F32)
+        if first:
+            load(2).wait()
         out = dot3(ti_ref, ab_s[...])
         low = out[0:32] - pltpu.roll(out[64:96], 64, 1)
         high = pltpu.roll(out[32:64], 64, 1) - out[96:128]
@@ -202,7 +216,7 @@
             q_s[pl.ds(pl.multiple_of(8 * i, 8), 8), :] = dot(moved, weights)
             return carry
 
-        lax.fori_loop(0, 16, step, 0, unroll=2)
+        lax.fori_loop(0, 16, step, 0, unroll=UNROLL)
         q_s[128:136, :] = dot(l_s[128:136, :].astype(BF16), kv[64])
         q_s[136:144, :] = jnp.zeros((8, 256), F32)
         out = dot3(ts_ref, q_s[...])
@@ -320,7 +334,17 @@
                 total = total - jnp.where(linked[k][r], v[2 * k + r], 0.0)
             dt_s[8 * r : 8 * r + 8] = total.reshape(8, 8, ROW)
 
+    load(0).wait()
+    load(1).wait()
     first_sum = forward(x0_ref[...], True)
+    prepare()
+    own = cell * (2 * ROW) + lax.broadcasted_iota(jnp.int32, (1, 2 * ROW), 1)
+    linked = [[None, None] for _ in range(4)]
+    for k in range(4):
+        both = jnp.where(nb_ref[pl.ds(k, 1), :] != own, 1.0, 0.0)
+        linked[k][0] = both[:, :ROW] > 0.5
+        linked[k][1] = both[:, ROW:] > 0.5
+    load(6).wait()
     pl.semaphore_wait(barrier, len(everyone))
     sum_start(0, first_sum)
     send(x0_ref.at[:, pl.ds(ROW, ROW)], h_n.at[pl.ds(0, 64)], nxt_id, h_ssem.at[0], h_rsem.at[0])
@@ -336,6 +360,8 @@
     start = start + [h_n[64:128], h_s[64:128]]
     divergence(start)
     jumps(jump_s, h_n[0:64], x0_ref[:, 0:ROW], x0_ref[:, ROW:], h_s[0:64])
+    for i in (7, 8, 9):
+        load(i).wait()
     observed = jnp.concatenate([obs_ref[0:32], obs_ref[32:64]], axis=1)
     misfit = sum_end(0) - observed
 
@@ -396,6 +422,8 @@
     size = step_size(1)
     est_ref[:, 0:ROW] = est_ref[:, 0:ROW] - size * g_s[1, 0:8].reshape(NT, ROW)
     est_ref[:, ROW:] = est_ref[:, ROW:] - size * g_s[1, 8:16].reshape(NT, ROW)
+    outs = [pltpu.make_async_copy(est_ref, est_hbm, out_sem.at[8])]
+    outs[0].start()
     for i in range(8):
         shifted = jump_s[i] - size * gj_s[i] + mult_s[i]
         limit = thresholds[i % 2]
@@ -403,7 +431,13 @@
         k, r = i // 2, i % 2
         aux_ref[k, :, r * ROW : (r + 1) * ROW] = shrunk
         mul_ref[k, :, r * ROW : (r + 1) * ROW] = shifted - shrunk
-
+        if r == 1:
+            for n, (src, dst) in enumerate(((aux_ref, aux_hbm), (mul_ref, mul_hbm))):
+                outs.append(pltpu.make_async_copy(src.at[k], dst.at[k], out_sem.at[4 * n + k]))
+                outs[-1].start()
+
+    for copy in outs:
+        copy.wait()
     wait_for(h_n, h_ssem.at[0])
     wait_for(h_s, h_ssem.at[1])
     for n in range(3):
@@ -421,22 +455,52 @@
         wait_for(gh_s.at[n], gh_ssem.at[n, 1])
 
 
+def finish(est, aux, mul, est_out, aux_out, mul_out, est_v, aux_v, mul_v, sems):
+    moves = ((aux, aux_v, aux_out), (mul, mul_v, mul_out), (est, est_v, est_out))
+    arriving = [
+        pltpu.make_async_copy(src, mid, sems.at[0, i]) for i, (src, mid, _) in enumerate(moves)
+    ]
+    leaving = [
+        pltpu.make_async_copy(mid, dst, sems.at[1, i]) for i, (_, mid, dst) in enumerate(moves)
+    ]
+    for copy in arriving:
+        copy.start()
+    for first, second in zip(arriving, leaving):
+        first.wait()
+        second.start()
+    for copy in leaving:
+        copy.wait()
+
+
 def per_device(kernel, observed, start_model, start_multiplier, neighbours, tile, weight):
-    vmem = pl.BlockSpec(memory_space=pltpu.VMEM)
+    hbm = pl.BlockSpec(memory_space=pltpu.HBM)
     scratch = lambda *shape, dtype=F32: pltpu.VMEM(shape, dtype)
     dma = lambda *shape: pltpu.SemaphoreType.DMA(shape)
     analysis, back, synthesis, closing = (jnp.asarray(t) for t in tables())
-    return pl.pallas_call(
+    results = pl.pallas_call(
         body,
         out_shape=(
             jax.ShapeDtypeStruct((NT, 256), F32),
             jax.ShapeDtypeStruct((4, NT, 256), F32),
             jax.ShapeDtypeStruct((4, NT, 256), F32),
         ),
-        in_specs=[pl.BlockSpec(memory_space=pl.ANY)] + [vmem] * 10,
-        out_specs=(vmem, vmem, vmem),
+        in_specs=[hbm] * 11,
+        out_specs=(hbm, hbm, hbm),
         scratch_shapes=[
             scratch(NF, 128, 256, dtype=BF16),
+            scratch(NT, 256),
+            scratch(4, NT, 256),
+            scratch(4, NT, 256),
+            scratch(NT, 64),
+            scratch(NT, 256),
+            scratch(4, NT, 256),
+            scratch(4, 256, dtype=jnp.int32),
+            scratch(1, 256, dtype=jnp.int32),
+            scratch(1, 64),
+            scratch(ROWS, 256, dtype=BF16),
+            scratch(2 * ROWS, 256, dtype=BF16),
+            scratch(2, 128, ROWS, dtype=BF16),
+            scratch(2, NT, ROWS, dtype=BF16),
             scratch(ROWS, 256),
             scratch(ROWS, ROW),
             scratch(ROWS, ROW),
@@ -468,6 +532,8 @@
             scratch(8, NT, ROW),
             scratch(8, NT, ROW),
             dma(2, 4),
+            dma(10),
+            dma(9),
             dma(2),
             dma(2),
             dma(3, 4),
@@ -482,13 +548,22 @@
             dma(2, 2),
         ],
         compiler_params=pltpu.CompilerParams(
-            collective_id=0, has_side_effects=True, vmem_limit_bytes=48 * 1024 * 1024
+            collective_id=0, has_side_effects=True, vmem_limit_bytes=MAIN_VMEM
         ),
         name="inversion",
     )(
         kernel, observed, start_model, start_multiplier, neighbours, tile.reshape(1, 256),
         weight.reshape(1, 64), analysis, back, synthesis, closing,
     )
+    return pl.pallas_call(
+        finish,
+        out_shape=tuple(jax.ShapeDtypeStruct(r.shape, F32) for r in results),
+        in_specs=[hbm] * 3,
+        out_specs=(hbm, hbm, hbm),
+        scratch_shapes=[pltpu.VMEM(r.shape, F32) for r in results] + [dma(2, 3)],
+        compiler_params=pltpu.CompilerParams(vmem_limit_bytes=MAIN_VMEM),
+        name="finish",
+    )(*results)
 
 
 def solution(mesh):

time: 89.5 us -> 75.9 us (0.85)
  local copies, waits for them, and re-layouts: 12.3 us -> 0 us
  Pallas kernels: 76 us -> 75.1 us
    unnamed x25 -> x0, local copies, waits for them, and re-layouts: 12.3 us -> none
    pallas_call x1, Pallas kernels: 76 us -> 73.3 us  [per_device(): pl.pallas_call(body, out_shape=(jax.ShapeDtypeStruct((NT, 256), F32), jax...]
    pallas_call x0 -> x1, Pallas kernels: none -> 1.8 us  [per_device(): pl.pallas_call(finish, out_shape=tuple((jax.ShapeDtypeStruct(r.shape, F32...]
where the time goes in v2:
time: 75.9 us; the launch traced here: 75.7 us
  Pallas kernels  75.1 us (99%)
    pallas_call x1, Pallas kernels, per_device(): pl.pallas_call(body, out_shape=(jax.ShapeDtypeStruct((NT, 256), F32), jax...  73.3 us
    pallas_call x1, Pallas kernels, per_device(): pl.pallas_call(finish, out_shape=tuple((jax.ShapeDtypeStruct(r.shape, F32...  1.8 us

profile of v2, /device:TPU:1, one launch (start us, length us, event | category | flops | bytes accessed | tf_op | source)
XLA Modules:
  0.0 75.7 jit_solution(10620104785254967519)
XLA Ops:
  0.6 73.3 %inversion.1 = (f32[64,256]{1,0:T(8,128)}, f32[4,64,256]{2,1,0:T(8,128)}, f32[4,64,256]{2,1,0:T(8,128)}) custom-call(bf16[2,65,64,256]{3,2,1,0:T(8,128)(2,1)} %k_hbm.1, f32[64,64]{1,0:T(8,128)} %obs_hbm.1, f32[64,256]{1,0:T(8,128)} %x0_hbm.1, f32[4,64,256]{2,1,0:T(8,128)} %m0_hbm.1, s32[4,256]{1,0:T(4,128)} %nb_hbm.1, s32[1,256]{1,0:T(1,128)} %bitcast.2, ...), custom_call_target="tpu_custom_call" | custom-call | tf_op jit(solution)/shard_map/inversion/pallas_call | solution.py:480
  73.9 1.8 %finish.1 = (f32[64,256]{1,0:T(8,128)}, f32[4,64,256]{2,1,0:T(8,128)}, f32[4,64,256]{2,1,0:T(8,128)}) custom-call(f32[64,256]{1,0:T(8,128)} %get-tuple-element.6.est, f32[4,64,256]{2,1,0:T(8,128)} %get-tuple-element.7.aux, f32[4,64,256]{2,1,0:T(8,128)} %get-tuple-element.8.mul), custom_call_target="tpu_custom_call" | custom-call | tf_op jit(solution)/shard_map/finish/pallas_call | solution.py:558

commit v3 on v2

--- a/solution.py
+++ b/solution.py
@@ -19,7 +19,7 @@
 SHRINK_SCALE = 0.4
 TINY = 1e-06
 UNROLL = 16
-MAIN_VMEM = 67043328
+MAIN_VMEM = 40 * 1024 * 1024
 F32 = jnp.float32
 BF16 = jnp.bfloat16
 MESH = pl.DeviceIdType.MESH
@@ -84,13 +84,13 @@
 
 def body(
     k_hbm, obs_hbm, x0_hbm, m0_hbm, nb_hbm, tile_hbm, w_hbm, tf_hbm, ta_hbm, ti_hbm, ts_hbm,
-    est_hbm, aux_hbm, mul_hbm,
-    kv, est_ref, aux_ref, mul_ref, obs_ref, x0_ref, m0_ref, nb_ref, tile_ref, w_ref, tf_ref, ta_ref, ti_ref, ts_ref, m_s, ab_s, l_s, q_s,
+    est_ref, aux_ref, mul_ref,
+    kv, obs_ref, x0_ref, m0_ref, nb_ref, tile_ref, w_ref, tf_ref, ta_ref, ti_ref, ts_ref, m_s, ab_s, l_s, q_s,
     send1, ya, zb, za, yb, mid_a, mid_b,
     sc_send, sc_mid, sy, sz, rs_send, rs_buf,
-    gp, rs_in, g_s, b_s, dt_s, thr_s, h_n, h_s, gh_n, gh_s,
+    gp, rs_in, g_s, b_s, dt_s, thr_s, h_m, h_t, hx_n, hx_s, gh_n, gh_s,
     jump_s, gj_s, mult_s,
-    k_sem, in_sem, out_sem, h_ssem, h_rsem, ar_ssem, ar_rsem, sc_ssem, sc_rsem, rs_ssem, rs_rsem, gr_ssem, gr_rsem,
+    k_sem, in_sem, h_ssem, h_rsem, ar_ssem, ar_rsem, sc_ssem, sc_rsem, rs_ssem, rs_rsem, gr_ssem, gr_rsem,
     gh_ssem, gh_rsem,
 ):
     my = lax.axis_index("y")
@@ -105,6 +105,11 @@
     z_ids = [{"zh": (mz + j) % NZ} for j in Z_ORDER]
     s_nums = [(ms + j) % NSEN for j in (7, 9, 6, 10, 5, 11, 4, 12, 3, 13, 8, 2, 14, 1, 15)]
 
+    tb = ms % 8
+    half = ms // 8
+    edge = (cell + NY * NZ + 1 - 2 * half) % (NY * NZ)
+    edge_id = {"y": edge // NZ, "zh": edge % NZ}
+
     def load(i):
         src, dst = loads[i]
         return pltpu.make_async_copy(src, dst, in_sem.at[i])
@@ -115,11 +120,6 @@
     )
     load(0).start()
     load(1).start()
-
-    barrier = pltpu.get_barrier_semaphore()
-    everyone = y_ids + z_ids + [{"sensor": p} for p in s_nums] + [nxt_id, prv_id]
-    for who in everyone:
-        pl.semaphore_signal(barrier, inc=1, device_id=who, device_id_type=MESH)
 
     bounds = (0, 16, 32, 48, 65)
 
@@ -134,6 +134,11 @@
     for q in range(4):
         for plane in range(2):
             k_copy(plane, q).start()
+    barrier = pltpu.get_barrier_semaphore()
+    everyone = y_ids + z_ids + [{"sensor": p} for p in s_nums] + [nxt_id, prv_id]
+    for who in everyone:
+        pl.semaphore_signal(barrier, inc=1, device_id=who, device_id_type=MESH)
+
     for i in range(2, 10):
         load(i).start()
 
@@ -324,12 +329,12 @@
 
     def divergence(v):
         for r in range(2):
-            from_south = v[5] if r == 0 else v[9]
-            from_north = v[8] if r == 0 else v[6]
             total = jnp.where(linked[1][r], pltpu.roll(v[r], 1, 1), 0.0)
             total = total + jnp.where(linked[0][r], pltpu.roll(v[2 + r], ROW - 1, 1), 0.0)
-            total = total + jnp.where(linked[3][r], from_south, 0.0)
-            total = total + jnp.where(linked[2][r], from_north, 0.0)
+            if r == 0:
+                total = total + jnp.where(linked[3][0], v[5], 0.0)
+            else:
+                total = total + jnp.where(linked[2][1], v[6], 0.0)
             for k in range(4):
                 total = total - jnp.where(linked[k][r], v[2 * k + r], 0.0)
             dt_s[8 * r : 8 * r + 8] = total.reshape(8, 8, ROW)
@@ -340,26 +345,26 @@
     prepare()
     own = cell * (2 * ROW) + lax.broadcasted_iota(jnp.int32, (1, 2 * ROW), 1)
     linked = [[None, None] for _ in range(4)]
+    edges = []
     for k in range(4):
         both = jnp.where(nb_ref[pl.ds(k, 1), :] != own, 1.0, 0.0)
         linked[k][0] = both[:, :ROW] > 0.5
         linked[k][1] = both[:, ROW:] > 0.5
+        if k >= 2:
+            edges.append(both[:, :ROW] if k == 2 else both[:, ROW:])
+    edge_link = jnp.where(half == 0, edges[0], edges[1]) > 0.5
     load(6).wait()
     pl.semaphore_wait(barrier, len(everyone))
     sum_start(0, first_sum)
-    send(x0_ref.at[:, pl.ds(ROW, ROW)], h_n.at[pl.ds(0, 64)], nxt_id, h_ssem.at[0], h_rsem.at[0])
-    send(m0_ref.at[3, :, pl.ds(ROW, ROW)], h_n.at[pl.ds(64, 64)], nxt_id, h_ssem.at[0], h_rsem.at[0])
-    send(thr_s.at[1], h_n.at[pl.ds(128, 8)], nxt_id, h_ssem.at[0], h_rsem.at[0])
-    send(x0_ref.at[:, pl.ds(0, ROW)], h_s.at[pl.ds(0, 64)], prv_id, h_ssem.at[1], h_rsem.at[1])
-    send(m0_ref.at[2, :, pl.ds(0, ROW)], h_s.at[pl.ds(64, 64)], prv_id, h_ssem.at[1], h_rsem.at[1])
-    send(thr_s.at[0], h_s.at[pl.ds(128, 8)], prv_id, h_ssem.at[1], h_rsem.at[1])
     sum_middle(0)
-    wait_for(h_n, h_rsem.at[0])
-    wait_for(h_s, h_rsem.at[1])
-    start = [m0_ref[k, :, r * ROW : (r + 1) * ROW] for k in range(4) for r in range(2)]
-    start = start + [h_n[64:128], h_s[64:128]]
-    divergence(start)
-    jumps(jump_s, h_n[0:64], x0_ref[:, 0:ROW], x0_ref[:, ROW:], h_s[0:64])
+    lanes = pl.multiple_of(ROW * (1 - half), ROW)
+    times = pl.multiple_of(8 * tb, 8)
+    send(
+        m0_ref.at[3 - half, pl.ds(times, 8), pl.ds(lanes, ROW)], h_m, edge_id,
+        h_ssem.at[0], h_rsem.at[0],
+    )
+    send(thr_s.at[1 - half], h_t, edge_id, h_ssem.at[1], h_rsem.at[1])
+    divergence([m0_ref[k, :, r * ROW : (r + 1) * ROW] for k in range(4) for r in range(2)])
     for i in (7, 8, 9):
         load(i).wait()
     observed = jnp.concatenate([obs_ref[0:32], obs_ref[32:64]], axis=1)
@@ -367,9 +372,14 @@
 
     adjoint(misfit, gp.at[0])
     scatter_start(0)
+    send(x0_ref.at[:, pl.ds(ROW, ROW)], hx_n, nxt_id, h_ssem.at[2], h_rsem.at[2])
+    send(x0_ref.at[:, pl.ds(0, ROW)], hx_s, prv_id, h_ssem.at[3], h_rsem.at[3])
+    wait_for(h_m, h_rsem.at[0])
+    wait_for(h_t, h_rsem.at[1])
+    extra = dt_s[ms] + jnp.where(edge_link, h_m[...], 0.0)
     piece = scatter_end(0)
     b_s[0] = piece
-    grad_a, grad_b = gather(0, piece + dt_s[ms])
+    grad_a, grad_b = gather(0, piece + extra)
     part = forward(jnp.concatenate([grad_a, grad_b], axis=1), False)
     sum_start(1, part)
     above, below = halo(0)
@@ -383,32 +393,32 @@
     response_start(0, response)
     adjoint(response, gp.at[1])
     scatter_start(1)
+    wait_for(hx_n, h_rsem.at[2])
+    wait_for(hx_s, h_rsem.at[3])
+    jumps(jump_s, hx_n[...], x0_ref[:, 0:ROW], x0_ref[:, ROW:], hx_s[...])
     size = step_size(0)
     penalty = []
-    thresholds = [thr_s[0, 0:1], thr_s[1, 0:1], h_n[128:129], h_s[128:129]]
-    for i in range(10):
-        if i < 8:
-            moved = jump_s[i] - size * gj_s[i]
-            limit = thresholds[i % 2]
-            held = m0_ref[i // 2, :, (i % 2) * ROW : (i % 2 + 1) * ROW]
-            jump_s[i] = moved
-        else:
-            source = 4 if i == 8 else 7
-            moved = -jump_s[source]
-            limit = thresholds[i - 6]
-            held = h_n[64:128] if i == 8 else h_s[64:128]
-        shifted = moved + held
+    thresholds = [thr_s[0, 0:1], thr_s[1, 0:1]]
+    for i in range(8):
+        moved = jump_s[i] - size * gj_s[i]
+        jump_s[i] = moved
+        limit = thresholds[i % 2]
+        shifted = moved + m0_ref[i // 2, :, (i % 2) * ROW : (i % 2 + 1) * ROW]
         shrunk = jnp.maximum(shifted - limit, 0.0) - jnp.maximum(-shifted - limit, 0.0)
         rest = shifted - shrunk
-        if i < 8:
-            mult_s[i] = rest
+        mult_s[i] = rest
         penalty.append(moved - shrunk + rest)
     divergence(penalty)
+    moved = -jump_s[4 + 3 * half, pl.ds(times, 8), :]
+    shifted = moved + h_m[...]
+    limit = h_t[...]
+    shrunk = jnp.maximum(shifted - limit, 0.0) - jnp.maximum(-shifted - limit, 0.0)
+    extra = dt_s[ms] + jnp.where(edge_link, moved - shrunk + (shifted - shrunk), 0.0)
     est_ref[:, 0:ROW] = x0_ref[:, 0:ROW] - size * g_s[0, 0:8].reshape(NT, ROW)
     est_ref[:, ROW:] = x0_ref[:, ROW:] - size * g_s[0, 8:16].reshape(NT, ROW)
 
     piece = b_s[0] - size * scatter_end(1)
-    grad_a, grad_b = gather(1, piece + dt_s[ms])
+    grad_a, grad_b = gather(1, piece + extra)
     part = forward(jnp.concatenate([grad_a, grad_b], axis=1), False)
     sum_start(2, part)
     above, below = halo(1)
@@ -422,8 +432,6 @@
     size = step_size(1)
     est_ref[:, 0:ROW] = est_ref[:, 0:ROW] - size * g_s[1, 0:8].reshape(NT, ROW)
     est_ref[:, ROW:] = est_ref[:, ROW:] - size * g_s[1, 8:16].reshape(NT, ROW)
-    outs = [pltpu.make_async_copy(est_ref, est_hbm, out_sem.at[8])]
-    outs[0].start()
     for i in range(8):
         shifted = jump_s[i] - size * gj_s[i] + mult_s[i]
         limit = thresholds[i % 2]
@@ -431,15 +439,9 @@
         k, r = i // 2, i % 2
         aux_ref[k, :, r * ROW : (r + 1) * ROW] = shrunk
         mul_ref[k, :, r * ROW : (r + 1) * ROW] = shifted - shrunk
-        if r == 1:
-            for n, (src, dst) in enumerate(((aux_ref, aux_hbm), (mul_ref, mul_hbm))):
-                outs.append(pltpu.make_async_copy(src.at[k], dst.at[k], out_sem.at[4 * n + k]))
-                outs[-1].start()
-
-    for copy in outs:
-        copy.wait()
-    wait_for(h_n, h_ssem.at[0])
-    wait_for(h_s, h_ssem.at[1])
+
+    for i, view in enumerate((h_m, h_t, hx_n, hx_s)):
+        wait_for(view, h_ssem.at[i])
     for n in range(3):
         wait_for(ya.at[n, pl.ds(0, NY - 1)], ar_ssem.at[n, 0])
         wait_for(zb.at[n, pl.ds(0, NZ - 1)], ar_ssem.at[n, 1])
@@ -455,28 +457,27 @@
         wait_for(gh_s.at[n], gh_ssem.at[n, 1])
 
 
-def finish(est, aux, mul, est_out, aux_out, mul_out, est_v, aux_v, mul_v, sems):
-    moves = ((aux, aux_v, aux_out), (mul, mul_v, mul_out), (est, est_v, est_out))
-    arriving = [
-        pltpu.make_async_copy(src, mid, sems.at[0, i]) for i, (src, mid, _) in enumerate(moves)
+def finish(est, aux, mul, est_out, aux_out, mul_out, sems):
+    copies = [
+        pltpu.make_async_copy(src, dst, sems.at[i])
+        for i, (src, dst) in enumerate(((aux, aux_out), (mul, mul_out), (est, est_out)))
     ]
-    leaving = [
-        pltpu.make_async_copy(mid, dst, sems.at[1, i]) for i, (_, mid, dst) in enumerate(moves)
-    ]
-    for copy in arriving:
+    for copy in copies:
         copy.start()
-    for first, second in zip(arriving, leaving):
-        first.wait()
-        second.start()
-    for copy in leaving:
+    for copy in copies:
         copy.wait()
 
 
 def per_device(kernel, observed, start_model, start_multiplier, neighbours, tile, weight):
     hbm = pl.BlockSpec(memory_space=pltpu.HBM)
+    vmem = pl.BlockSpec(memory_space=pltpu.VMEM)
     scratch = lambda *shape, dtype=F32: pltpu.VMEM(shape, dtype)
     dma = lambda *shape: pltpu.SemaphoreType.DMA(shape)
     analysis, back, synthesis, closing = (jnp.asarray(t) for t in tables())
+    inputs = (
+        kernel, observed, start_model, start_multiplier, neighbours, tile.reshape(1, 256),
+        weight.reshape(1, 64), analysis, back, synthesis, closing,
+    )
     results = pl.pallas_call(
         body,
         out_shape=(
@@ -485,12 +486,9 @@
             jax.ShapeDtypeStruct((4, NT, 256), F32),
         ),
         in_specs=[hbm] * 11,
-        out_specs=(hbm, hbm, hbm),
+        out_specs=(vmem, vmem, vmem),
         scratch_shapes=[
             scratch(NF, 128, 256, dtype=BF16),
-            scratch(NT, 256),
-            scratch(4, NT, 256),
-            scratch(4, NT, 256),
             scratch(NT, 64),
             scratch(NT, 256),
             scratch(4, NT, 256),
@@ -524,8 +522,10 @@
             scratch(3, 8, ROW),
             scratch(16, 8, ROW),
             scratch(2, 8, ROW),
-            scratch(136, ROW),
-            scratch(136, ROW),
+            scratch(8, ROW),
+            scratch(8, ROW),
+            scratch(NT, ROW),
+            scratch(NT, ROW),
             scratch(2, 8, 8, ROW),
             scratch(2, 8, 8, ROW),
             scratch(8, NT, ROW),
@@ -533,9 +533,8 @@
             scratch(8, NT, ROW),
             dma(2, 4),
             dma(10),
-            dma(9),
-            dma(2),
-            dma(2),
+            dma(4),
+            dma(4),
             dma(3, 4),
             dma(3, 4),
             dma(2, 2),
@@ -551,17 +550,14 @@
             collective_id=0, has_side_effects=True, vmem_limit_bytes=MAIN_VMEM
         ),
         name="inversion",
-    )(
-        kernel, observed, start_model, start_multiplier, neighbours, tile.reshape(1, 256),
-        weight.reshape(1, 64), analysis, back, synthesis, closing,
-    )
+    )(*(pltpu.with_memory_space_constraint(x, pltpu.HBM) for x in inputs))
     return pl.pallas_call(
         finish,
         out_shape=tuple(jax.ShapeDtypeStruct(r.shape, F32) for r in results),
-        in_specs=[hbm] * 3,
+        in_specs=[vmem] * 3,
         out_specs=(hbm, hbm, hbm),
-        scratch_shapes=[pltpu.VMEM(r.shape, F32) for r in results] + [dma(2, 3)],
-        compiler_params=pltpu.CompilerParams(vmem_limit_bytes=MAIN_VMEM),
+        scratch_shapes=[dma(3)],
+        compiler_params=pltpu.CompilerParams(vmem_limit_bytes=1024 * 1024),
         name="finish",
     )(*results)
 

time: 75.9 us -> 72.7 us (0.958)
  Pallas kernels: 75.1 us -> 72 us
    pallas_call x1, Pallas kernels: 73.3 us -> 71.1 us  [per_device(): pl.pallas_call(body, out_shape=(jax.ShapeDtypeStruct((NT, 256), F32), jax...]
    pallas_call x1, Pallas kernels: 1.8 us -> 0.83 us  [per_device(): pl.pallas_call(finish, out_shape=tuple((jax.ShapeDtypeStruct(r.shape, F32...]
where the time goes in v3:
time: 72.7 us; the launch traced here: 72.6 us
  Pallas kernels  72 us (99%)
    pallas_call x1, Pallas kernels, per_device(): pl.pallas_call(body, out_shape=(jax.ShapeDtypeStruct((NT, 256), F32), jax...  71.1 us

profile of v3, /device:TPU:1, one launch (start us, length us, event | category | flops | bytes accessed | tf_op | source)
XLA Modules:
  0.0 72.6 jit_solution(15929241416706121446)
XLA Ops:
  0.6 71.1 %inversion.1 = (f32[64,256]{1,0:T(8,128)S(1)}, f32[4,64,256]{2,1,0:T(8,128)S(1)}, f32[4,64,256]{2,1,0:T(8,128)S(1)}) custom-call(bf16[2,65,64,256]{3,2,1,0:T(8,128)(2,1)} %k_hbm.1, f32[64,64]{1,0:T(8,128)} %obs_hbm.1, f32[64,256]{1,0:T(8,128)} %x0_hbm.1, f32[4,64,256]{2,1,0:T(8,128)} %m0_hbm.1, s32[4,256]{1,0:T(4,128)} %nb_hbm.1, s32[1,256]{1,0:T(1,128)} %bitcast.2, ...), custom_call_target="tpu_custom_call" | custom-call | tf_op jit(solution)/shard_map/inversion/pallas_call | solution.py:481
  71.8 0.8 %finish.1 = (f32[64,256]{1,0:T(8,128)}, f32[4,64,256]{2,1,0:T(8,128)}, f32[4,64,256]{2,1,0:T(8,128)}) custom-call(f32[64,256]{1,0:T(8,128)S(1)} %get-tuple-element.6.est, f32[4,64,256]{2,1,0:T(8,128)S(1)} %get-tuple-element.7.aux, f32[4,64,256]{2,1,0:T(8,128)S(1)} %get-tuple-element.8.mul), custom_call_target="tpu_custom_call" | custom-call | tf_op jit(solution)/shard_map/finish/pallas_call | solution.py:554

commit v4 on v3

--- a/solution.py
+++ b/solution.py
@@ -18,7 +18,6 @@
 ROWS = 144
 SHRINK_SCALE = 0.4
 TINY = 1e-06
-UNROLL = 16
 MAIN_VMEM = 40 * 1024 * 1024
 F32 = jnp.float32
 BF16 = jnp.bfloat16
@@ -121,7 +120,7 @@
     load(0).start()
     load(1).start()
 
-    bounds = (0, 16, 32, 48, 65)
+    bounds = (0, 16, 32, 48, 56, 65)
 
     def k_copy(plane, q):
         lo, hi = bounds[q], bounds[q + 1]
@@ -131,7 +130,7 @@
             k_sem.at[plane, q],
         )
 
-    for q in range(4):
+    for q in range(len(bounds) - 1):
         for plane in range(2):
             k_copy(plane, q).start()
     barrier = pltpu.get_barrier_semaphore()
@@ -174,37 +173,58 @@
 
     group_row = lax.broadcasted_iota(jnp.int32, (8, ROW), 0) // 2
 
-    def forward(field, first):
-        m_s[...] = dot(tf_ref[...], stacked(field))
+    def block_rows(i):
+        return pl.ds(pl.multiple_of(8 * i, 8), 8)
+
+    def own_rows(out):
+        kept = out[:, 0:ROW]
+        for j in range(1, 4):
+            kept = jnp.where(group_row == j, out[:, j * ROW : (j + 1) * ROW], kept)
+        return kept
+
+    def cells(h):
+        return pl.ds(pl.multiple_of(ROW * h, ROW), ROW)
+
+    def forward_start(field):
+        for h in range(2):
+            m_s[h] = dot(tf_ref[...], stacked(field[:, h * ROW : (h + 1) * ROW]))
 
         def step(i, carry):
-            moved = m_s[pl.ds(pl.multiple_of(8 * i, 8), 8), :].astype(BF16)
+            moved = jnp.concatenate([m_s[0, block_rows(i), :], m_s[1, block_rows(i), :]], axis=1)
             weights = kv[pl.ds(4 * i, 4)].reshape(512, 256)
-            out = dot(moved, weights, ((1,), (1,)))
-            kept = out[:, 0:ROW]
-            for j in range(1, 4):
-                kept = jnp.where(group_row == j, out[:, j * ROW : (j + 1) * ROW], kept)
-            ab_s[pl.ds(pl.multiple_of(8 * i, 8), 8), :] = kept
+            ab_s[block_rows(i), :] = own_rows(dot(moved.astype(BF16), weights, ((1,), (1,))))
             return carry
 
-        if first:
-            for q in range(4):
-                k_copy(0, q).wait()
-                k_copy(1, q).wait()
-                lax.fori_loop(4 * q, 4 * q + 4, step, 0, unroll=4)
-        else:
-            lax.fori_loop(0, 16, step, 0, unroll=UNROLL)
-        tail = m_s[128:136, :].astype(BF16)
+        for q in range(len(bounds) - 1):
+            k_copy(0, q).wait()
+            k_copy(1, q).wait()
+            lo, hi = bounds[q] // 4, min(bounds[q + 1] // 4, 16)
+            lax.fori_loop(lo, hi, step, 0, unroll=hi - lo)
+        tail = jnp.concatenate([m_s[0, 128:136, :], m_s[1, 128:136, :]], axis=1).astype(BF16)
         ab_s[128:136, :] = dot(tail, kv[64], ((1,), (1,)))
         ab_s[136:144, :] = jnp.zeros((8, ROW), F32)
-        if first:
-            load(2).wait()
+
+    def forward_half(field, h, adds):
+        m_s[h] = dot(tf_ref[...], stacked(field))
+
+        def step(i, carry):
+            moved = m_s[h, block_rows(i), :].astype(BF16)
+            weights = kv[pl.ds(4 * i, 4), :, cells(h)].reshape(512, ROW)
+            kept = own_rows(dot(moved, weights, ((1,), (1,))))
+            ab_s[block_rows(i), :] = ab_s[block_rows(i), :] + kept if adds else kept
+            return carry
+
+        lax.fori_loop(0, 16, step, 0, unroll=16)
+        tail = dot(m_s[h, 128:136, :].astype(BF16), kv[64, :, cells(h)], ((1,), (1,)))
+        ab_s[128:136, :] = ab_s[128:136, :] + tail if adds else tail
+
+    def forward_end():
         out = dot3(ti_ref, ab_s[...])
         low = out[0:32] - pltpu.roll(out[64:96], 64, 1)
         high = pltpu.roll(out[32:64], 64, 1) - out[96:128]
         return jnp.where(left_half, low, high)
 
-    def adjoint(packed, dst):
+    def adjoint(packed, n):
         turned = pltpu.roll(packed, 64, 1)
         doubled = jnp.concatenate(
             [jnp.where(left_half, packed, turned), jnp.where(left_half, turned, packed)], axis=0
@@ -212,21 +232,26 @@
         out = dot(ta_ref[...], stacked(doubled))
         l_s[...] = jnp.where(left_half, out[:ROWS], out[ROWS:])
 
-        def step(i, carry):
-            rows = l_s[pl.ds(pl.multiple_of(8 * i, 8), 8), :]
-            moved = jnp.concatenate(
-                [jnp.where(group_row == j, rows, 0.0) for j in range(4)], axis=1
-            ).astype(BF16)
-            weights = kv[pl.ds(4 * i, 4)].reshape(512, 256)
-            q_s[pl.ds(pl.multiple_of(8 * i, 8), 8), :] = dot(moved, weights)
-            return carry
-
-        lax.fori_loop(0, 16, step, 0, unroll=UNROLL)
-        q_s[128:136, :] = dot(l_s[128:136, :].astype(BF16), kv[64])
-        q_s[136:144, :] = jnp.zeros((8, 256), F32)
-        out = dot3(ts_ref, q_s[...])
-        dst[0:8] = out[:, :ROW].reshape(8, 8, ROW)
-        dst[8:16] = out[:, ROW:].reshape(8, 8, ROW)
+        for h, order in ((1 - half, (4, 3, 5, 2, 6, 1, 7, 0)), (half, (4, 3, 5, 2, 6, 1, 7))):
+
+            def step(i, carry):
+                rows = l_s[block_rows(i), :]
+                moved = jnp.concatenate(
+                    [jnp.where(group_row == j, rows, 0.0) for j in range(4)], axis=1
+                ).astype(BF16)
+                weights = kv[pl.ds(4 * i, 4), :, cells(h)].reshape(512, ROW)
+                q_s[h, block_rows(i), :] = dot(moved, weights)
+                return carry
+
+            lax.fori_loop(0, 16, step, 0, unroll=16)
+            q_s[h, 128:136, :] = dot(l_s[128:136, :].astype(BF16), kv[64, :, cells(h)])
+            q_s[h, 136:144, :] = jnp.zeros((8, ROW), F32)
+            out = dot3(ts_ref, q_s[h])
+            gp[n, pl.ds(8 * h, 8)] = out.reshape(8, 8, ROW)
+            for j in order:
+                p = 8 * h + (tb + j) % 8
+                send(gp.at[n, p], rs_in.at[n, ms], {"sensor": p}, gr_ssem.at[n, 0], gr_rsem.at[n, 0])
+        rs_in[n, ms] = gp[n, ms]
 
     def sum_start(n, packed):
         send1[n] = packed
@@ -287,24 +312,27 @@
         response = jnp.sum(jnp.sum(rs_buf[n], axis=0), axis=1, keepdims=True)
         return total[0:1] / (response + total[1:2] + TINY)
 
-    def scatter_start(n):
-        rs_in[n, ms] = gp[n, ms]
-        for p in s_nums:
-            send(gp.at[n, p], rs_in.at[n, ms], {"sensor": p}, gr_ssem.at[n, 0], gr_rsem.at[n, 0])
-
     def scatter_end(n):
         wait_for(rs_in.at[n, pl.ds(0, NSEN - 1)], gr_rsem.at[n, 0])
         return jnp.sum(rs_in[n], axis=0)
 
-    def gather(n, piece):
+    def gather_forward(n, piece):
         b_s[1 + n] = piece
         g_s[n, ms] = piece
-        for p in s_nums:
-            send(b_s.at[1 + n], g_s.at[n, ms], {"sensor": p}, gr_ssem.at[n, 1], gr_rsem.at[n, 1])
-        wait_for(g_s.at[n, pl.ds(0, NSEN - 1)], gr_rsem.at[n, 1])
+        src, dst = b_s.at[1 + n], g_s.at[n, ms]
+        for j in (4, 3, 5, 2, 6, 1, 7, 0):
+            who = {"sensor": 8 * (1 - half) + (tb + j) % 8}
+            send(src, dst, who, gr_ssem.at[n, 1], gr_rsem.at[n, 1])
+        for j in (4, 3, 5, 2, 6, 1, 7):
+            who = {"sensor": 8 * half + (tb + j) % 8}
+            send(src, dst, who, gr_ssem.at[n, 2], gr_rsem.at[n, 2])
+        wait_for(g_s.at[n, pl.ds(0, 7)], gr_rsem.at[n, 2])
+        forward_half(g_s[n, pl.ds(8 * half, 8)].reshape(NT, ROW), half, False)
+        wait_for(g_s.at[n, pl.ds(0, 8)], gr_rsem.at[n, 1])
         send(g_s.at[n, pl.ds(8, 8)], gh_n.at[n], nxt_id, gh_ssem.at[n, 0], gh_rsem.at[n, 0])
         send(g_s.at[n, pl.ds(0, 8)], gh_s.at[n], prv_id, gh_ssem.at[n, 1], gh_rsem.at[n, 1])
-        return g_s[n, 0:8].reshape(NT, ROW), g_s[n, 8:16].reshape(NT, ROW)
+        forward_half(g_s[n, pl.ds(8 * (1 - half), 8)].reshape(NT, ROW), 1 - half, True)
+        return forward_end()
 
     def halo(n):
         wait_for(gh_n.at[n], gh_rsem.at[n, 0])
@@ -341,7 +369,11 @@
 
     load(0).wait()
     load(1).wait()
-    first_sum = forward(x0_ref[...], True)
+    forward_start(x0_ref[...])
+    load(2).wait()
+    first_sum = forward_end()
+    pl.semaphore_wait(barrier, len(everyone))
+    sum_start(0, first_sum)
     prepare()
     own = cell * (2 * ROW) + lax.broadcasted_iota(jnp.int32, (1, 2 * ROW), 1)
     linked = [[None, None] for _ in range(4)]
@@ -354,8 +386,6 @@
             edges.append(both[:, :ROW] if k == 2 else both[:, ROW:])
     edge_link = jnp.where(half == 0, edges[0], edges[1]) > 0.5
     load(6).wait()
-    pl.semaphore_wait(barrier, len(everyone))
-    sum_start(0, first_sum)
     sum_middle(0)
     lanes = pl.multiple_of(ROW * (1 - half), ROW)
     times = pl.multiple_of(8 * tb, 8)
@@ -370,8 +400,7 @@
     observed = jnp.concatenate([obs_ref[0:32], obs_ref[32:64]], axis=1)
     misfit = sum_end(0) - observed
 
-    adjoint(misfit, gp.at[0])
-    scatter_start(0)
+    adjoint(misfit, 0)
     send(x0_ref.at[:, pl.ds(ROW, ROW)], hx_n, nxt_id, h_ssem.at[2], h_rsem.at[2])
     send(x0_ref.at[:, pl.ds(0, ROW)], hx_s, prv_id, h_ssem.at[3], h_rsem.at[3])
     wait_for(h_m, h_rsem.at[0])
@@ -379,9 +408,7 @@
     extra = dt_s[ms] + jnp.where(edge_link, h_m[...], 0.0)
     piece = scatter_end(0)
     b_s[0] = piece
-    grad_a, grad_b = gather(0, piece + extra)
-    part = forward(jnp.concatenate([grad_a, grad_b], axis=1), False)
-    sum_start(1, part)
+    sum_start(1, gather_forward(0, piece + extra))
     above, below = halo(0)
     grad_a = g_s[0, 0:8].reshape(NT, ROW)
     grad_b = g_s[0, 8:16].reshape(NT, ROW)
@@ -391,8 +418,7 @@
     scalars_middle(0)
     response = sum_end(1)
     response_start(0, response)
-    adjoint(response, gp.at[1])
-    scatter_start(1)
+    adjoint(response, 1)
     wait_for(hx_n, h_rsem.at[2])
     wait_for(hx_s, h_rsem.at[3])
     jumps(jump_s, hx_n[...], x0_ref[:, 0:ROW], x0_ref[:, ROW:], hx_s[...])
@@ -418,9 +444,7 @@
     est_ref[:, ROW:] = x0_ref[:, ROW:] - size * g_s[0, 8:16].reshape(NT, ROW)
 
     piece = b_s[0] - size * scatter_end(1)
-    grad_a, grad_b = gather(1, piece + extra)
-    part = forward(jnp.concatenate([grad_a, grad_b], axis=1), False)
-    sum_start(2, part)
+    sum_start(2, gather_forward(1, piece + extra))
     above, below = halo(1)
     grad_a = g_s[1, 0:8].reshape(NT, ROW)
     grad_b = g_s[1, 8:16].reshape(NT, ROW)
@@ -452,7 +476,8 @@
         wait_for(sz.at[n, pl.ds(0, NZ - 1)], sc_ssem.at[n, 1])
         wait_for(rs_buf.at[n, pl.ds(0, NSEN - 1)], rs_ssem.at[n])
         wait_for(rs_in.at[n, pl.ds(0, NSEN - 1)], gr_ssem.at[n, 0])
-        wait_for(g_s.at[n, pl.ds(0, NSEN - 1)], gr_ssem.at[n, 1])
+        wait_for(g_s.at[n, pl.ds(0, 8)], gr_ssem.at[n, 1])
+        wait_for(g_s.at[n, pl.ds(0, 7)], gr_ssem.at[n, 2])
         wait_for(gh_n.at[n], gh_ssem.at[n, 0])
         wait_for(gh_s.at[n], gh_ssem.at[n, 1])
 
@@ -499,10 +524,10 @@
             scratch(2 * ROWS, 256, dtype=BF16),
             scratch(2, 128, ROWS, dtype=BF16),
             scratch(2, NT, ROWS, dtype=BF16),
-            scratch(ROWS, 256),
+            scratch(2, ROWS, ROW),
             scratch(ROWS, ROW),
             scratch(ROWS, ROW),
-            scratch(ROWS, 256),
+            scratch(2, ROWS, ROW),
             scratch(3, 32, ROW),
             scratch(3, NY, 16, ROW),
             scratch(3, NZ, 16, ROW),
@@ -531,7 +556,7 @@
             scratch(8, NT, ROW),
             scratch(8, NT, ROW),
             scratch(8, NT, ROW),
-            dma(2, 4),
+            dma(2, 5),
             dma(10),
             dma(4),
             dma(4),
@@ -541,8 +566,8 @@
             dma(2, 2),
             dma(2),
             dma(2),
-            dma(2, 2),
-            dma(2, 2),
+            dma(2, 3),
+            dma(2, 3),
             dma(2, 2),
             dma(2, 2),
         ],

time: 72.7 us -> 72.2 us (level)
  no operation moved by 1% of the time
where the time goes in v4:
time: 72.2 us; the launch traced here: 72.1 us
  Pallas kernels  71.4 us (99%)
    pallas_call x1, Pallas kernels, per_device(): pl.pallas_call(body, out_shape=(jax.ShapeDtypeStruct((NT, 256), F32), jax...  70.6 us

profile of v4, /device:TPU:1, one launch (start us, length us, event | category | flops | bytes accessed | tf_op | source)
XLA Modules:
  0.0 72.1 jit_solution(7324330343032942701)
XLA Ops:
  0.6 70.6 %inversion.1 = (f32[64,256]{1,0:T(8,128)S(1)}, f32[4,64,256]{2,1,0:T(8,128)S(1)}, f32[4,64,256]{2,1,0:T(8,128)S(1)}) custom-call(bf16[2,65,64,256]{3,2,1,0:T(8,128)(2,1)} %k_hbm.1, f32[64,64]{1,0:T(8,128)} %obs_hbm.1, f32[64,256]{1,0:T(8,128)} %x0_hbm.1, f32[4,64,256]{2,1,0:T(8,128)} %m0_hbm.1, s32[4,256]{1,0:T(4,128)} %nb_hbm.1, s32[1,256]{1,0:T(1,128)} %bitcast.2, ...), custom_call_target="tpu_custom_call" | custom-call | tf_op jit(solution)/shard_map/inversion/pallas_call | solution.py:506
  71.2 0.8 %finish.1 = (f32[64,256]{1,0:T(8,128)}, f32[4,64,256]{2,1,0:T(8,128)}, f32[4,64,256]{2,1,0:T(8,128)}) custom-call(f32[64,256]{1,0:T(8,128)S(1)} %get-tuple-element.6.est, f32[4,64,256]{2,1,0:T(8,128)S(1)} %get-tuple-element.7.aux, f32[4,64,256]{2,1,0:T(8,128)S(1)} %get-tuple-element.8.mul), custom_call_target="tpu_custom_call" | custom-call | tf_op jit(solution)/shard_map/finish/pallas_call | solution.py:579

commit v5 on v4

--- a/solution.py
+++ b/solution.py
@@ -130,14 +130,14 @@
             k_sem.at[plane, q],
         )
 
-    for q in range(len(bounds) - 1):
-        for plane in range(2):
-            k_copy(plane, q).start()
     barrier = pltpu.get_barrier_semaphore()
     everyone = y_ids + z_ids + [{"sensor": p} for p in s_nums] + [nxt_id, prv_id]
     for who in everyone:
         pl.semaphore_signal(barrier, inc=1, device_id=who, device_id_type=MESH)
 
+    for q in range(len(bounds) - 1):
+        for plane in range(2):
+            k_copy(plane, q).start()
     for i in range(2, 10):
         load(i).start()
 

time: 72.2 us -> 71.5 us (level)
    pallas_call x1, Pallas kernels: 70.6 us -> 69.8 us  [per_device(): pl.pallas_call(body, out_shape=(jax.ShapeDtypeStruct((NT, 256), F32), jax...]
where the time goes in v5:
time: 71.5 us; the launch traced here: 71.3 us
  Pallas kernels  70.7 us (99%)
    pallas_call x1, Pallas kernels, per_device(): pl.pallas_call(body, out_shape=(jax.ShapeDtypeStruct((NT, 256), F32), jax...  69.8 us

profile of v5, /device:TPU:1, one launch (start us, length us, event | category | flops | bytes accessed | tf_op | source)
XLA Modules:
  0.0 71.3 jit_solution(18149241356226166727)
XLA Ops:
  0.6 69.8 %inversion.1 = (f32[64,256]{1,0:T(8,128)S(1)}, f32[4,64,256]{2,1,0:T(8,128)S(1)}, f32[4,64,256]{2,1,0:T(8,128)S(1)}) custom-call(bf16[2,65,64,256]{3,2,1,0:T(8,128)(2,1)} %k_hbm.1, f32[64,64]{1,0:T(8,128)} %obs_hbm.1, f32[64,256]{1,0:T(8,128)} %x0_hbm.1, f32[4,64,256]{2,1,0:T(8,128)} %m0_hbm.1, s32[4,256]{1,0:T(4,128)} %nb_hbm.1, s32[1,256]{1,0:T(1,128)} %bitcast.2, ...), custom_call_target="tpu_custom_call" | custom-call | tf_op jit(solution)/shard_map/inversion/pallas_call | solution.py:506
  70.5 0.8 %finish.1 = (f32[64,256]{1,0:T(8,128)}, f32[4,64,256]{2,1,0:T(8,128)}, f32[4,64,256]{2,1,0:T(8,128)}) custom-call(f32[64,256]{1,0:T(8,128)S(1)} %get-tuple-element.6.est, f32[4,64,256]{2,1,0:T(8,128)S(1)} %get-tuple-element.7.aux, f32[4,64,256]{2,1,0:T(8,128)S(1)} %get-tuple-element.8.mul), custom_call_target="tpu_custom_call" | custom-call | tf_op jit(solution)/shard_map/finish/pallas_call | solution.py:579
